TPU v7x, 512 devices: a whole 4x8x8 slice. The times are simulated.
512 devices in a mesh: grp: 8 (over y_lo, x), view: 64 (over y_hi, z, core).
Axes of the slice: x: 4, y: 8 (y_hi: 4, y_lo: 2; y = y_hi * 2 + y_lo), z: 8, core: 2. Of those that a mesh axis runs over, the one named last changes fastest.
Arguments:
- volume: float32 [1024, 16, 2, 512], P(('grp', 'view')), may hold values from 0 to 2
- footprint: bfloat16 [1024, 2, 512, 896], P(('grp', 'view')), may hold values from -0.1875 to 0.1875
- measured: bfloat16 [4096, 64, 896], P(('grp', 'view')), may hold values from 0 to 3
- angle_index: int32 [4096], P(('grp', 'view')), may hold values from 0 to 1
- cover: int32 [4096, 4], P(('grp', 'view')), may hold values from 0 to 1023, as said below
- offset: int32 [4096, 4], P(('grp', 'view')), may hold values from 0 to 48
- count: int32 [4096], P(('grp', 'view')), may hold values from 1 to 4
Outputs:
- gradient: float32 [1024, 16, 2, 512], P(('grp', 'view'))
Inputs may be any that keep to these rules, and one draw needn't show every extreme that they name: Let p = v // 8. cover[v,k] lies between max(p - 4, 0) * 2 and min(p + 5, 512) * 2 - 1, and both ends are named by some slot 0 of p's views.
All inputs are finite; a program needn't handle non-finite values.
Results may differ from a plain program's by a relative error of at most 0.0019.
Values may be sent and summed in bfloat16 or wider, within the bound.
A program may use at most 64 MiB of HBM per device.

v0:
```python
import jax
import jax.numpy as jnp
from jax import lax
from jax.sharding import PartitionSpec as P

REACH = 4


DELTA = 0.5
PRIOR_WEIGHT = 2.0


def passed_along(shard, axis, by):
    peers = lax.axis_size(axis)
    pairs = [(i, i + by) for i in range(peers) if 0 <= i + by < peers]
    return lax.ppermute(shard, axis, pairs)


def padded_2(block, sides, width):
    for axis, dim in sides:
        count = lax.axis_size(axis)
        forward = [(i, i + 1) for i in range(count - 1)]
        backward = [(target, source) for source, target in forward]
        low = lax.ppermute(
            lax.slice_in_dim(block, block.shape[dim] - width, None, axis=dim), axis, forward
        )
        high = lax.ppermute(lax.slice_in_dim(block, 0, width, axis=dim), axis, backward)
        block = jnp.concatenate([low, block, high], axis=dim)
    return block


def shards(volume, footprint, measured, angle_index, cover, offset, count):
    local_blocks, slab_rows, strip_rows, row_width = volume.shape
    view_count, det_rows, channels = measured.shape
    table_count = footprint.shape[0]
    slot_count = cover.shape[1]
    plane = strip_rows * row_width
    total_dev = lax.axis_size(("grp", "view"))
    position = lax.axis_index(("grp", "view"))
    vol_bf = volume.astype(jnp.bfloat16)
    pieces = []
    for step in range(-REACH, REACH + 1):
        if step == 0:
            pieces.append(vol_bf)
        else:
            pieces.append(passed_along(vol_bf, ("grp", "view"), -step))
    window = jnp.concatenate(pieces, 0)
    win_blocks = window.shape[0]
    win_rows = window.reshape(win_blocks * slab_rows, plane)
    tables = footprint.reshape(table_count, plane, channels)
    base = (position - REACH) * local_blocks
    highest = lax.Precision.HIGHEST
    table_proj = jnp.stack(
        [
            jnp.dot(win_rows, tables[table], preferred_element_type=jnp.float32)
            for table in range(table_count)
        ],
        0,
    )
    table_proj = table_proj.reshape(table_count * win_blocks, slab_rows * channels)
    local_idx = cover - base
    slot_iota = jnp.arange(slot_count, dtype=jnp.int32)
    alive = (slot_iota[None, :] < count[:, None]).astype(jnp.float32)
    pick_key = angle_index[:, None] * win_blocks + local_idx
    select = (
        pick_key[:, :, None] == jnp.arange(table_count * win_blocks, dtype=jnp.int32)[None, None, :]
    ).astype(jnp.float32)
    gathered = jnp.dot(
        select.reshape(view_count * slot_count, table_count * win_blocks),
        table_proj,
        precision=highest,
        preferred_element_type=jnp.float32,
    )
    gathered = gathered.reshape(view_count, slot_count, slab_rows, channels)
    row_target = offset[:, :, None] + jnp.arange(slab_rows, dtype=jnp.int32)[None, None, :]
    row_hit = (
        row_target[:, :, :, None] == jnp.arange(det_rows, dtype=jnp.int32)[None, None, None, :]
    ).astype(jnp.float32)
    placing = row_hit * alive[:, :, None, None]
    forward_projection = jnp.einsum(
        "vkir,vkic->vrc", placing, gathered, precision=highest, preferred_element_type=jnp.float32
    )
    measured_float = measured.astype(jnp.float32)
    weighted_residual = (jnp.exp(-measured_float) * (forward_projection - measured_float)).astype(
        jnp.bfloat16
    )
    picked = jnp.einsum(
        "vkir,vrc->vkic",
        row_hit.astype(jnp.bfloat16),
        weighted_residual,
        preferred_element_type=jnp.float32,
    ).astype(jnp.bfloat16)
    back = jnp.zeros((view_count * slot_count * slab_rows, plane), jnp.float32)
    for table in range(table_count):
        table_mask = (angle_index == table).astype(jnp.bfloat16)[:, None, None, None]
        masked = (picked * table_mask).reshape(view_count * slot_count * slab_rows, channels)
        back = back + lax.dot_general(
            masked, tables[table], (((1,), (1,)), ((), ())), preferred_element_type=jnp.float32
        )
    back = back.reshape(view_count * slot_count, slab_rows * plane)
    scatter_rows = (
        local_idx[:, :, None] == jnp.arange(win_blocks, dtype=jnp.int32)[None, None, :]
    ).astype(jnp.float32) * alive[:, :, None]
    scatter_rows = scatter_rows.reshape(view_count * slot_count, win_blocks)
    win_grad = lax.dot_general(
        scatter_rows,
        back,
        (((0,), (0,)), ((), ())),
        precision=highest,
        preferred_element_type=jnp.float32,
    )
    parts = win_grad.reshape((2 * REACH + 1, local_blocks, slab_rows, strip_rows, row_width))
    data_grad = parts[REACH]
    for step in range(-REACH, REACH + 1):
        if step != 0:
            data_grad = data_grad + passed_along(parts[REACH + step], ("grp", "view"), step)
    slices_here = local_blocks * slab_rows
    flat = volume.reshape(slices_here, strip_rows, row_width)
    padded = padded_2(flat, ((("grp", "view"), 0),), 1)
    global_row = position * slices_here + jnp.arange(slices_here, dtype=jnp.int32)
    lower_ok = (global_row > 0)[:, None, None]
    upper_ok = (global_row < total_dev * slices_here - 1)[:, None, None]
    prior = jnp.where(lower_ok, jnp.clip(flat - padded[:-2], -DELTA, DELTA), 0.0)
    prior = prior + jnp.where(upper_ok, jnp.clip(flat - padded[2:], -DELTA, DELTA), 0.0)
    ydiff = jnp.clip(flat[:, 1:] - flat[:, :-1], -DELTA, DELTA)
    prior = (
        prior + jnp.pad(ydiff, ((0, 0), (1, 0), (0, 0))) - jnp.pad(ydiff, ((0, 0), (0, 1), (0, 0)))
    )
    xdiff = jnp.clip(flat[:, :, 1:] - flat[:, :, :-1], -DELTA, DELTA)
    prior = (
        prior + jnp.pad(xdiff, ((0, 0), (0, 0), (1, 0))) - jnp.pad(xdiff, ((0, 0), (0, 0), (0, 1)))
    )
    return data_grad + PRIOR_WEIGHT * prior.reshape(volume.shape)


def solution(mesh):
    in_specs = (
        P(("grp", "view"), None, None, None),
        P(("grp", "view"), None, None, None),
        P(("grp", "view"), None, None),
        P(("grp", "view")),
        P(("grp", "view"), None),
        P(("grp", "view"), None),
        P(("grp", "view")),
    )
    out_specs = P(("grp", "view"), None, None, None)
    return jax.shard_map(shards, mesh=mesh, in_specs=in_specs, out_specs=out_specs, check_vma=False)
```

profile of v0, /device:TPU:8, one launch (start us, length us, event | category | flops | bytes accessed | tf_op | source)
XLA Modules:
  0.0 117.1 jit_solution(10478743159029252121)
XLA Ops:
  0.0 0.9 convert_element_type.56
  1.0 6.1 %collective-permute-start = (bf16[2,16,2,512]{3,2,1,0:T(2,128)(2,1)S(1)}, bf16[2,16,2,512]{3,2,1,0:T(2,128)(2,1)S(1)}, u32[]{:S(2)}, u32[]{:S(2)}) collective-permute-start(bf16[2,16,2,512]{3,2,1,0:T(2,128)(2,1)S(1)} %convert_element_type.56), channel_id=1, source_target_pairs={{0,4},{1,5},{2,6},{3,7},{4,8},{5,9},{6,10},{7,11},{8,12},{9,13},{1... | collective-permute-start | bytes 196616 | tf_op jit(solution)/shard_map/ppermute | solution.py:16
  7.0 3.4 %collective-permute-start.1 = (bf16[2,16,2,512]{3,2,1,0:T(2,128)(2,1)S(1)}, bf16[2,16,2,512]{3,2,1,0:T(2,128)(2,1)S(1)}, u32[]{:S(2)}, u32[]{:S(2)}) collective-permute-start(bf16[2,16,2,512]{3,2,1,0:T(2,128)(2,1)S(1)} %convert_element_type.56), channel_id=1, source_target_pairs={{0,3},{1,4},{2,5},{3,6},{4,7},{5,8},{6,9},{7,10},{8,11},{9,12},{10... | collective-permute-start | bytes 196616 | tf_op jit(solution)/shard_map/ppermute | solution.py:16
  10.5 5.5 %collective-permute-start.2 = (bf16[2,16,2,512]{3,2,1,0:T(2,128)(2,1)S(1)}, bf16[2,16,2,512]{3,2,1,0:T(2,128)(2,1)S(1)}, u32[]{:S(2)}, u32[]{:S(2)}) collective-permute-start(bf16[2,16,2,512]{3,2,1,0:T(2,128)(2,1)S(1)} %convert_element_type.56), channel_id=1, source_target_pairs={{0,2},{1,3},{2,4},{3,5},{4,6},{5,7},{6,8},{7,9},{8,10},{9,11},{10,... | collective-permute-start | bytes 196616 | tf_op jit(solution)/shard_map/ppermute | solution.py:16
  16.0 3.5 %collective-permute-start.3 = (bf16[2,16,2,512]{3,2,1,0:T(2,128)(2,1)S(1)}, bf16[2,16,2,512]{3,2,1,0:T(2,128)(2,1)S(1)}, u32[]{:S(2)}, u32[]{:S(2)}) collective-permute-start(bf16[2,16,2,512]{3,2,1,0:T(2,128)(2,1)S(1)} %convert_element_type.56), channel_id=1, source_target_pairs={{0,1},{1,2},{2,3},{3,4},{4,5},{5,6},{6,7},{7,8},{8,9},{9,10},{10,1... | collective-permute-start | bytes 196616 | tf_op jit(solution)/shard_map/ppermute | solution.py:16
  19.5 9.3 %collective-permute-start.4 = (bf16[2,16,2,512]{3,2,1,0:T(2,128)(2,1)S(1)}, bf16[2,16,2,512]{3,2,1,0:T(2,128)(2,1)S(1)}, u32[]{:S(2)}, u32[]{:S(2)}) collective-permute-start(bf16[2,16,2,512]{3,2,1,0:T(2,128)(2,1)S(1)} %convert_element_type.56), channel_id=1, source_target_pairs={{1,0},{2,1},{3,2},{4,3},{5,4},{6,5},{7,6},{8,7},{9,8},{10,9},{11,1... | collective-permute-start | bytes 196616 | tf_op jit(solution)/shard_map/ppermute | solution.py:16
  28.8 0.7 fusion.42
  29.5 1.2 %fusion.13 = f32[32,2,511]{2,1,0:T(2,128)S(1)} fusion(f32[32,2,512]{2,1,0:T(2,128)} %bitcast.60), kind=kLoop, calls=%fused_computation.22 | loop fusion | flops 65408 | bytes 392448 | tf_op jit(solution)/shard_map/jit(clip)/min | solution.py:129
  30.8 3.6 %fusion.40 = (bf16[1,2,512,896]{3,2,1,0:T(8,128)(2,1)}, bf16[1,2,512,896]{3,2,1,0:T(8,128)(2,1)S(1)}) fusion(bf16[2,2,512,896]{3,2,1,0:T(8,128)(2,1)} %param.8), kind=kLoop, calls=%fused_computation.72 | loop fusion | bytes 7340032 | tf_op jit(solution)/shard_map/slice | solution.py:55
  34.4 0.1 copy.12
  34.5 0.1 iota_add_fusion
  34.6 0.1 fusion.35
  34.7 0.1 copy.11
  34.8 0.1 eq.65
  34.8 0.1 reshape.142
  34.9 2.3 %collective-permute-start.5 = (bf16[2,16,2,512]{3,2,1,0:T(2,128)(2,1)S(1)}, bf16[2,16,2,512]{3,2,1,0:T(2,128)(2,1)S(1)}, u32[]{:S(2)}, u32[]{:S(2)}) collective-permute-start(bf16[2,16,2,512]{3,2,1,0:T(2,128)(2,1)S(1)} %convert_element_type.56), channel_id=1, source_target_pairs={{2,0},{3,1},{4,2},{5,3},{6,4},{7,5},{8,6},{9,7},{10,8},{11,9},{12,... | collective-permute-start | bytes 196616 | tf_op jit(solution)/shard_map/ppermute | solution.py:16
  37.3 1.9 %collective-permute-start.6 = (bf16[2,16,2,512]{3,2,1,0:T(2,128)(2,1)S(1)}, bf16[2,16,2,512]{3,2,1,0:T(2,128)(2,1)S(1)}, u32[]{:S(2)}, u32[]{:S(2)}) collective-permute-start(bf16[2,16,2,512]{3,2,1,0:T(2,128)(2,1)S(1)} %convert_element_type.56), channel_id=1, source_target_pairs={{3,0},{4,1},{5,2},{6,3},{7,4},{8,5},{9,6},{10,7},{11,8},{12,9},{13... | collective-permute-start | bytes 196616 | tf_op jit(solution)/shard_map/ppermute | solution.py:16
  39.2 0.1 constant_dynamic-update-slice_fusion.7
  39.3 5.1 %collective-permute-start.7 = (bf16[2,16,2,512]{3,2,1,0:T(2,128)(2,1)S(1)}, bf16[2,16,2,512]{3,2,1,0:T(2,128)(2,1)S(1)}, u32[]{:S(2)}, u32[]{:S(2)}) collective-permute-start(bf16[2,16,2,512]{3,2,1,0:T(2,128)(2,1)S(1)} %convert_element_type.56), channel_id=1, source_target_pairs={{4,0},{5,1},{6,2},{7,3},{8,4},{9,5},{10,6},{11,7},{12,8},{13,9},{1... | collective-permute-start | bytes 196616 | tf_op jit(solution)/shard_map/ppermute | solution.py:16
  44.4 0.1 constant_dynamic-update-slice_fusion.6
  44.5 2.6 %collective-permute-start.16 = (f32[1,2,512]{2,1,0:T(2,128)S(1)}, f32[1,2,512]{2,1,0:T(2,128)S(1)}, u32[]{:S(2)}, u32[]{:S(2)}) collective-permute-start(f32[1,2,512]{2,1,0:T(2,128)S(1)} %get-tuple-element.20), channel_id=1, source_target_pairs={{0,1},{1,2},{2,3},{3,4},{4,5},{5,6},{6,7},{7,8},{8,9},{9,10},{10,1... | collective-permute-start | bytes 12296 | tf_op jit(solution)/shard_map/ppermute | solution.py:24
  47.1 0.1 constant_dynamic-update-slice_fusion.5
  47.2 10.2 %collective-permute-start.17 = (f32[1,2,512]{2,1,0:T(2,128)S(1)}, f32[1,2,512]{2,1,0:T(2,128)S(1)}, u32[]{:S(2)}, u32[]{:S(2)}) collective-permute-start(f32[1,2,512]{2,1,0:T(2,128)S(1)} %get-tuple-element.21), channel_id=1, source_target_pairs={{1,0},{2,1},{3,2},{4,3},{5,4},{6,5},{7,6},{8,7},{9,8},{10,9},{11,1... | collective-permute-start | bytes 12296 | tf_op jit(solution)/shard_map/ppermute | solution.py:27
  57.5 0.1 constant_dynamic-update-slice_fusion.3
  57.7 0.1 copy.18
  57.8 0.8 convolution_bitcast_fusion
  58.6 0.7 copy-done.3
  59.3 0.8 convolution_bitcast_fusion.1
  60.1 1.5 %pad_maximum_fusion = f32[2,288,896]{2,1,0:T(8,128)} fusion(f32[1,288,896]{2,1,0:T(8,128)S(1)} %convolution_bitcast_fusion, f32[1,288,896]{2,1,0:T(8,128)S(1)} %convolution_bitcast_fusion.1), kind=kLoop, calls=%fused_computation.5 | loop fusion | flops 516096 | bytes 4128768 | tf_op jit(solution)/shard_map/stack | solution.py:53
  61.6 1.7 %reshape.137 = f32[36,14336]{1,0:T(8,128)S(1)} reshape(f32[2,288,896]{2,1,0:T(8,128)} %pad_maximum_fusion) | data formatting | bytes 4128768 | tf_op jit(solution)/shard_map/reshape | solution.py:60
  63.3 0.4 copy.19
  63.8 0.1 slice_bitcast_fusion
  63.9 1.8 %fusion = f32[8,4,16,896]{3,0,2,1:T(8,128)S(1)} fusion(f32[16,896,36,1]{1,0,2,3:T(8,128)S(1)} %slice_bitcast_fusion, s32[8,4]{0,1:T(4,128)S(1)} %get-tuple-element.5), kind=kOutput, calls=%fused_computation | convolution fusion | flops 198182016 | bytes 3899520 | tf_op jit(solution)/shard_map/dot_general | solution.py:68
  65.8 2.3 %fusion.9 = bf16[8,64,896,1]{2,1,3,0:T(8,128)(2,1)S(1)} fusion(f32[8,4,16,896]{3,0,2,1:T(8,128)S(1)} %fusion, bf16[8,64,896]{2,1,0:T(8,128)(2,1)S(1)} %copy-done.5, f32[8,4]{1,0:T(8,128)S(1)} %fusion.35, s32[8,4,16]{2,1,0:T(4,128)S(1)} %iota_add_fusion), kind=kOutput, calls=%fused_computation.15 | convolution fusion | flops 354680832 | bytes 3672192 | tf_op jit(solution)/shard_map/vkir,vkic->vrc/dot_general | solution.py:80
  68.1 0.5 broadcast_multiply_fusion
  68.5 1.0 copy-done.4
  69.6 1.3 %fusion.43 = f32[512,1024]{1,0:T(8,128)S(1)} fusion(bf16[512,896]{1,0:T(8,128)(2,1)S(1)} %bitcast.68, bf16[1024,896]{1,0:T(8,128)(2,1)S(1)} %bitcast.66), kind=kOutput, calls=%fused_computation.75 | convolution fusion | flops 939524096 | bytes 4849664 | tf_op jit(solution)/shard_map/dot_general | solution.py:97
  70.8 0.2 copy-done.2
  71.1 2.6 %convolution_add_fusion = f32[512,1024]{1,0:T(8,128)} fusion(f32[512,1024]{1,0:T(8,128)S(1)} %fusion.43, bf16[512,896]{1,0:T(8,128)(2,1)S(1)} %bitcast.67, bf16[1024,896]{1,0:T(8,128)(2,1)S(1)} %bitcast.64), kind=kOutput, calls=%fused_computation.11 | convolution fusion | flops 940048384 | bytes 6946816 | tf_op jit(solution)/shard_map/dot_general | solution.py:97
  73.7 1.7 %reshape.140 = f32[32,16384]{1,0:T(8,128)S(1)} reshape(f32[512,1024]{1,0:T(8,128)} %convolution_add_fusion) | data formatting | bytes 4194304 | tf_op jit(solution)/shard_map/reshape | solution.py:100
  75.4 1.6 %fusion.27 = f32[18,16384]{1,0:T(8,128)S(1)} fusion(f32[32,16384]{1,0:T(8,128)S(1)} %reshape.140, f32[32]{0:T(128)S(1)} %reshape.142, s32[32]{0:T(128)S(1)} %eq.65), kind=kOutput, calls=%fused_computation.52 | convolution fusion | flops 113247360 | bytes 3277056 | tf_op jit(solution)/shard_map/dot_general | solution.py:105
  77.1 0.4 fusion.41
  77.5 0.2 squeeze.45
  77.7 1.9 %collective-permute-start.15 = (f32[2,16,2,512]{3,2,1,0:T(2,128)S(1)}, f32[2,16,2,512]{3,2,1,0:T(2,128)S(1)}, u32[]{:S(2)}, u32[]{:S(2)}) collective-permute-start(f32[2,16,2,512]{3,2,1,0:T(2,128)S(1)} %squeeze.45), channel_id=1, source_target_pairs={{0,4},{1,5},{2,6},{3,7},{4,8},{5,9},{6,10},{7,11},{8,12},{9,13},{1... | collective-permute-start | bytes 393224 | tf_op jit(solution)/shard_map/ppermute | solution.py:16
  79.6 0.2 squeeze.44
  79.8 1.9 %collective-permute-start.14 = (f32[2,16,2,512]{3,2,1,0:T(2,128)S(1)}, f32[2,16,2,512]{3,2,1,0:T(2,128)S(1)}, u32[]{:S(2)}, u32[]{:S(2)}) collective-permute-start(f32[2,16,2,512]{3,2,1,0:T(2,128)S(1)} %squeeze.44), channel_id=1, source_target_pairs={{0,3},{1,4},{2,5},{3,6},{4,7},{5,8},{6,9},{7,10},{8,11},{9,12},{10... | collective-permute-start | bytes 393224 | tf_op jit(solution)/shard_map/ppermute | solution.py:16
  81.7 0.2 squeeze.43
  81.8 1.9 %collective-permute-start.13 = (f32[2,16,2,512]{3,2,1,0:T(2,128)S(1)}, f32[2,16,2,512]{3,2,1,0:T(2,128)S(1)}, u32[]{:S(2)}, u32[]{:S(2)}) collective-permute-start(f32[2,16,2,512]{3,2,1,0:T(2,128)S(1)} %squeeze.43), channel_id=1, source_target_pairs={{0,2},{1,3},{2,4},{3,5},{4,6},{5,7},{6,8},{7,9},{8,10},{9,11},{10,... | collective-permute-start | bytes 393224 | tf_op jit(solution)/shard_map/ppermute | solution.py:16
  83.8 0.1 fusion.26
  83.9 0.2 squeeze.42
  84.1 0.2 squeeze.41
  84.2 0.2 squeeze.40
  84.4 0.2 squeeze.39
  84.6 0.2 squeeze.38
  84.7 1.9 %collective-permute-start.12 = (f32[2,16,2,512]{3,2,1,0:T(2,128)S(1)}, f32[2,16,2,512]{3,2,1,0:T(2,128)S(1)}, u32[]{:S(2)}, u32[]{:S(2)}) collective-permute-start(f32[2,16,2,512]{3,2,1,0:T(2,128)S(1)} %squeeze.42), channel_id=1, source_target_pairs={{0,1},{1,2},{2,3},{3,4},{4,5},{5,6},{6,7},{7,8},{8,9},{9,10},{10,1... | collective-permute-start | bytes 393224 | tf_op jit(solution)/shard_map/ppermute | solution.py:16
  86.7 10.9 %collective-permute-start.11 = (f32[2,16,2,512]{3,2,1,0:T(2,128)S(1)}, f32[2,16,2,512]{3,2,1,0:T(2,128)S(1)}, u32[]{:S(2)}, u32[]{:S(2)}) collective-permute-start(f32[2,16,2,512]{3,2,1,0:T(2,128)S(1)} %squeeze.41), channel_id=1, source_target_pairs={{1,0},{2,1},{3,2},{4,3},{5,4},{6,5},{7,6},{8,7},{9,8},{10,9},{11,1... | collective-permute-start | bytes 393224 | tf_op jit(solution)/shard_map/ppermute | solution.py:16
  97.6 3.9 %collective-permute-start.10 = (f32[2,16,2,512]{3,2,1,0:T(2,128)S(1)}, f32[2,16,2,512]{3,2,1,0:T(2,128)S(1)}, u32[]{:S(2)}, u32[]{:S(2)}) collective-permute-start(f32[2,16,2,512]{3,2,1,0:T(2,128)S(1)} %squeeze.40), channel_id=1, source_target_pairs={{2,0},{3,1},{4,2},{5,3},{6,4},{7,5},{8,6},{9,7},{10,8},{11,9},{12,... | collective-permute-start | bytes 393224 | tf_op jit(solution)/shard_map/ppermute | solution.py:16
  101.5 2.9 %collective-permute-start.9 = (f32[2,16,2,512]{3,2,1,0:T(2,128)S(1)}, f32[2,16,2,512]{3,2,1,0:T(2,128)S(1)}, u32[]{:S(2)}, u32[]{:S(2)}) collective-permute-start(f32[2,16,2,512]{3,2,1,0:T(2,128)S(1)} %squeeze.39), channel_id=1, source_target_pairs={{3,0},{4,1},{5,2},{6,3},{7,4},{8,5},{9,6},{10,7},{11,8},{12,9},{13... | collective-permute-start | bytes 393224 | tf_op jit(solution)/shard_map/ppermute | solution.py:16
  104.4 5.9 %collective-permute-start.8 = (f32[2,16,2,512]{3,2,1,0:T(2,128)S(1)}, f32[2,16,2,512]{3,2,1,0:T(2,128)S(1)}, u32[]{:S(2)}, u32[]{:S(2)}) collective-permute-start(f32[2,16,2,512]{3,2,1,0:T(2,128)S(1)} %squeeze.38), channel_id=1, source_target_pairs={{4,0},{5,1},{6,2},{7,3},{8,4},{9,5},{10,6},{11,7},{12,8},{13,9},{1... | collective-permute-start | bytes 393224 | tf_op jit(solution)/shard_map/ppermute | solution.py:16
  110.3 0.4 subtract_multiply_fusion
  110.7 0.2 squeeze.37
  110.9 2.0 %collective-permute-done.9 = f32[2,16,2,512]{3,2,1,0:T(2,128)S(1)} collective-permute-done((f32[2,16,2,512]{3,2,1,0:T(2,128)S(1)}, f32[2,16,2,512]{3,2,1,0:T(2,128)S(1)}, u32[]{:S(2)}, u32[]{:S(2)}) %collective-permute-start.9) | collective-permute-done | bytes 131104 | tf_op jit(solution)/shard_map/ppermute | solution.py:16
  112.9 3.4 %collective-permute-done.8 = f32[2,16,2,512]{3,2,1,0:T(2,128)S(1)} collective-permute-done((f32[2,16,2,512]{3,2,1,0:T(2,128)S(1)}, f32[2,16,2,512]{3,2,1,0:T(2,128)S(1)}, u32[]{:S(2)}, u32[]{:S(2)}) %collective-permute-start.8) | collective-permute-done | bytes 131104 | tf_op jit(solution)/shard_map/ppermute | solution.py:16
  116.3 0.8 add_add_fusion
  (42 shorter events, 0.4 us)
Async XLA Ops:
  1.0 34.0 %collective-permute-start = (bf16[2,16,2,512]{3,2,1,0:T(2,128)(2,1)S(1)}, bf16[2,16,2,512]{3,2,1,0:T(2,128)(2,1)S(1)}, u32[]{:S(2)}, u32[]{:S(2)}) collective-permute-start(bf16[2,16,2,512]{3,2,1,0:T(2,128)(2,1)S(1)} %convert_element_type.56), channel_id=1, source_target_pairs={{0,4},{1,5},{2,6},{3,7},{4,8},{5,9},{6,10},{7,11},{8,12},{9,13},{1... | collective-permute-start | bytes 196616 | tf_op jit(solution)/shard_map/ppermute | solution.py:16
  7.0 30.2 %collective-permute-start.1 = (bf16[2,16,2,512]{3,2,1,0:T(2,128)(2,1)S(1)}, bf16[2,16,2,512]{3,2,1,0:T(2,128)(2,1)S(1)}, u32[]{:S(2)}, u32[]{:S(2)}) collective-permute-start(bf16[2,16,2,512]{3,2,1,0:T(2,128)(2,1)S(1)} %convert_element_type.56), channel_id=1, source_target_pairs={{0,3},{1,4},{2,5},{3,6},{4,7},{5,8},{6,9},{7,10},{8,11},{9,12},{10... | collective-permute-start | bytes 196616 | tf_op jit(solution)/shard_map/ppermute | solution.py:16
  10.5 28.8 %collective-permute-start.2 = (bf16[2,16,2,512]{3,2,1,0:T(2,128)(2,1)S(1)}, bf16[2,16,2,512]{3,2,1,0:T(2,128)(2,1)S(1)}, u32[]{:S(2)}, u32[]{:S(2)}) collective-permute-start(bf16[2,16,2,512]{3,2,1,0:T(2,128)(2,1)S(1)} %convert_element_type.56), channel_id=1, source_target_pairs={{0,2},{1,3},{2,4},{3,5},{4,6},{5,7},{6,8},{7,9},{8,10},{9,11},{10,... | collective-permute-start | bytes 196616 | tf_op jit(solution)/shard_map/ppermute | solution.py:16
  16.0 28.5 %collective-permute-start.3 = (bf16[2,16,2,512]{3,2,1,0:T(2,128)(2,1)S(1)}, bf16[2,16,2,512]{3,2,1,0:T(2,128)(2,1)S(1)}, u32[]{:S(2)}, u32[]{:S(2)}) collective-permute-start(bf16[2,16,2,512]{3,2,1,0:T(2,128)(2,1)S(1)} %convert_element_type.56), channel_id=1, source_target_pairs={{0,1},{1,2},{2,3},{3,4},{4,5},{5,6},{6,7},{7,8},{8,9},{9,10},{10,1... | collective-permute-start | bytes 196616 | tf_op jit(solution)/shard_map/ppermute | solution.py:16
  19.5 27.7 %collective-permute-start.4 = (bf16[2,16,2,512]{3,2,1,0:T(2,128)(2,1)S(1)}, bf16[2,16,2,512]{3,2,1,0:T(2,128)(2,1)S(1)}, u32[]{:S(2)}, u32[]{:S(2)}) collective-permute-start(bf16[2,16,2,512]{3,2,1,0:T(2,128)(2,1)S(1)} %convert_element_type.56), channel_id=1, source_target_pairs={{1,0},{2,1},{3,2},{4,3},{5,4},{6,5},{7,6},{8,7},{9,8},{10,9},{11,1... | collective-permute-start | bytes 196616 | tf_op jit(solution)/shard_map/ppermute | solution.py:16
  30.7 3.7 %copy-start.9 = (s32[8]{0:T(128)S(1)}, s32[8]{0:T(128)}, u32[]{:S(2)}) copy-start(s32[8]{0:T(128)} %param.10) | copy-start | bytes 100
  30.7 3.7 %copy-start.6 = (s32[8,4]{0,1:T(4,128)S(1)}, s32[8,4]{0,1:T(4,128)}, u32[]{:S(2)}) copy-start(s32[8,4]{0,1:T(4,128)} %param.12) | copy-start | bytes 388
  30.7 3.9 %copy-start.8 = (s32[8]{0:T(128)S(1)}, s32[8]{0:T(128)}, u32[]{:S(2)}) copy-start(s32[8]{0:T(128)} %param.13) | copy-start | bytes 100
  30.7 3.9 %copy-start.7 = (s32[8,4]{0,1:T(4,128)S(1)}, s32[8,4]{0,1:T(4,128)}, u32[]{:S(2)}) copy-start(s32[8,4]{0,1:T(4,128)} %param.11) | copy-start | bytes 388
  30.8 16.4 %copy-start = (f32[2,16,2,512]{3,2,1,0:T(2,128)S(1)}, f32[2,16,2,512]{3,2,1,0:T(2,128)}, u32[]{:S(2)}) copy-start(f32[2,16,2,512]{3,2,1,0:T(2,128)} %param.7) | copy-start | bytes 393220
  34.4 24.2 %copy-start.1 = (bf16[1,2,512,896]{3,2,1,0:T(8,128)(2,1)}, bf16[1,2,512,896]{3,2,1,0:T(8,128)(2,1)S(1)}, u32[]{:S(2)}) copy-start(bf16[1,2,512,896]{3,2,1,0:T(8,128)(2,1)S(1)} %get-tuple-element.8) | copy-start | bytes 5505028
  34.9 22.6 %collective-permute-start.5 = (bf16[2,16,2,512]{3,2,1,0:T(2,128)(2,1)S(1)}, bf16[2,16,2,512]{3,2,1,0:T(2,128)(2,1)S(1)}, u32[]{:S(2)}, u32[]{:S(2)}) collective-permute-start(bf16[2,16,2,512]{3,2,1,0:T(2,128)(2,1)S(1)} %convert_element_type.56), channel_id=1, source_target_pairs={{2,0},{3,1},{4,2},{5,3},{6,4},{7,5},{8,6},{9,7},{10,8},{11,9},{12,... | collective-permute-start | bytes 196616 | tf_op jit(solution)/shard_map/ppermute | solution.py:16
  37.3 20.3 %collective-permute-start.6 = (bf16[2,16,2,512]{3,2,1,0:T(2,128)(2,1)S(1)}, bf16[2,16,2,512]{3,2,1,0:T(2,128)(2,1)S(1)}, u32[]{:S(2)}, u32[]{:S(2)}) collective-permute-start(bf16[2,16,2,512]{3,2,1,0:T(2,128)(2,1)S(1)} %convert_element_type.56), channel_id=1, source_target_pairs={{3,0},{4,1},{5,2},{6,3},{7,4},{8,5},{9,6},{10,7},{11,8},{12,9},{13... | collective-permute-start | bytes 196616 | tf_op jit(solution)/shard_map/ppermute | solution.py:16
  39.3 18.4 %collective-permute-start.7 = (bf16[2,16,2,512]{3,2,1,0:T(2,128)(2,1)S(1)}, bf16[2,16,2,512]{3,2,1,0:T(2,128)(2,1)S(1)}, u32[]{:S(2)}, u32[]{:S(2)}) collective-permute-start(bf16[2,16,2,512]{3,2,1,0:T(2,128)(2,1)S(1)} %convert_element_type.56), channel_id=1, source_target_pairs={{4,0},{5,1},{6,2},{7,3},{8,4},{9,5},{10,6},{11,7},{12,8},{13,9},{1... | collective-permute-start | bytes 196616 | tf_op jit(solution)/shard_map/ppermute | solution.py:16
  44.5 40.2 %collective-permute-start.16 = (f32[1,2,512]{2,1,0:T(2,128)S(1)}, f32[1,2,512]{2,1,0:T(2,128)S(1)}, u32[]{:S(2)}, u32[]{:S(2)}) collective-permute-start(f32[1,2,512]{2,1,0:T(2,128)S(1)} %get-tuple-element.20), channel_id=1, source_target_pairs={{0,1},{1,2},{2,3},{3,4},{4,5},{5,6},{6,7},{7,8},{8,9},{9,10},{10,1... | collective-permute-start | bytes 12296 | tf_op jit(solution)/shard_map/ppermute | solution.py:24
  47.2 39.4 %collective-permute-start.17 = (f32[1,2,512]{2,1,0:T(2,128)S(1)}, f32[1,2,512]{2,1,0:T(2,128)S(1)}, u32[]{:S(2)}, u32[]{:S(2)}) collective-permute-start(f32[1,2,512]{2,1,0:T(2,128)S(1)} %get-tuple-element.21), channel_id=1, source_target_pairs={{1,0},{2,1},{3,2},{4,3},{5,4},{6,5},{7,6},{8,7},{9,8},{10,9},{11,1... | collective-permute-start | bytes 12296 | tf_op jit(solution)/shard_map/ppermute | solution.py:27
  57.8 1.5 %copy-start.3 = (bf16[1,2,512,896]{3,2,1,0:T(8,128)(2,1)S(1)}, bf16[1,2,512,896]{3,2,1,0:T(8,128)(2,1)}, u32[]{:S(2)}) copy-start(bf16[1,2,512,896]{3,2,1,0:T(8,128)(2,1)} %get-tuple-element.7) | copy-start | bytes 5505028
  63.9 1.8 %copy-start.5 = (bf16[8,64,896]{2,1,0:T(8,128)(2,1)S(1)}, bf16[8,64,896]{2,1,0:T(8,128)(2,1)}, u32[]{:S(2)}) copy-start(bf16[8,64,896]{2,1,0:T(8,128)(2,1)} %param.9) | copy-start | bytes 2752516
  68.1 1.5 %copy-start.4 = (bf16[1,2,512,896]{3,2,1,0:T(8,128)(2,1)S(1)}, bf16[1,2,512,896]{3,2,1,0:T(8,128)(2,1)}, u32[]{:S(2)}) copy-start(bf16[1,2,512,896]{3,2,1,0:T(8,128)(2,1)} %get-tuple-element.7) | copy-start | bytes 5505028
  69.6 1.5 %copy-start.2 = (bf16[1,2,512,896]{3,2,1,0:T(8,128)(2,1)S(1)}, bf16[1,2,512,896]{3,2,1,0:T(8,128)(2,1)}, u32[]{:S(2)}) copy-start(bf16[1,2,512,896]{3,2,1,0:T(8,128)(2,1)} %copy-done.1) | copy-start | bytes 5505028
  77.7 19.9 %collective-permute-start.15 = (f32[2,16,2,512]{3,2,1,0:T(2,128)S(1)}, f32[2,16,2,512]{3,2,1,0:T(2,128)S(1)}, u32[]{:S(2)}, u32[]{:S(2)}) collective-permute-start(f32[2,16,2,512]{3,2,1,0:T(2,128)S(1)} %squeeze.45), channel_id=1, source_target_pairs={{0,4},{1,5},{2,6},{3,7},{4,8},{5,9},{6,10},{7,11},{8,12},{9,13},{1... | collective-permute-start | bytes 393224 | tf_op jit(solution)/shard_map/ppermute | solution.py:16
  79.8 21.7 %collective-permute-start.14 = (f32[2,16,2,512]{3,2,1,0:T(2,128)S(1)}, f32[2,16,2,512]{3,2,1,0:T(2,128)S(1)}, u32[]{:S(2)}, u32[]{:S(2)}) collective-permute-start(f32[2,16,2,512]{3,2,1,0:T(2,128)S(1)} %squeeze.44), channel_id=1, source_target_pairs={{0,3},{1,4},{2,5},{3,6},{4,7},{5,8},{6,9},{7,10},{8,11},{9,12},{10... | collective-permute-start | bytes 393224 | tf_op jit(solution)/shard_map/ppermute | solution.py:16
  81.8 22.6 %collective-permute-start.13 = (f32[2,16,2,512]{3,2,1,0:T(2,128)S(1)}, f32[2,16,2,512]{3,2,1,0:T(2,128)S(1)}, u32[]{:S(2)}, u32[]{:S(2)}) collective-permute-start(f32[2,16,2,512]{3,2,1,0:T(2,128)S(1)} %squeeze.43), channel_id=1, source_target_pairs={{0,2},{1,3},{2,4},{3,5},{4,6},{5,7},{6,8},{7,9},{8,10},{9,11},{10,... | collective-permute-start | bytes 393224 | tf_op jit(solution)/shard_map/ppermute | solution.py:16
  84.7 26.1 %collective-permute-start.12 = (f32[2,16,2,512]{3,2,1,0:T(2,128)S(1)}, f32[2,16,2,512]{3,2,1,0:T(2,128)S(1)}, u32[]{:S(2)}, u32[]{:S(2)}) collective-permute-start(f32[2,16,2,512]{3,2,1,0:T(2,128)S(1)} %squeeze.42), channel_id=1, source_target_pairs={{0,1},{1,2},{2,3},{3,4},{4,5},{5,6},{6,7},{7,8},{8,9},{9,10},{10,1... | collective-permute-start | bytes 393224 | tf_op jit(solution)/shard_map/ppermute | solution.py:16
  86.7 24.2 %collective-permute-start.11 = (f32[2,16,2,512]{3,2,1,0:T(2,128)S(1)}, f32[2,16,2,512]{3,2,1,0:T(2,128)S(1)}, u32[]{:S(2)}, u32[]{:S(2)}) collective-permute-start(f32[2,16,2,512]{3,2,1,0:T(2,128)S(1)} %squeeze.41), channel_id=1, source_target_pairs={{1,0},{2,1},{3,2},{4,3},{5,4},{6,5},{7,6},{8,7},{9,8},{10,9},{11,1... | collective-permute-start | bytes 393224 | tf_op jit(solution)/shard_map/ppermute | solution.py:16
  97.6 13.3 %collective-permute-start.10 = (f32[2,16,2,512]{3,2,1,0:T(2,128)S(1)}, f32[2,16,2,512]{3,2,1,0:T(2,128)S(1)}, u32[]{:S(2)}, u32[]{:S(2)}) collective-permute-start(f32[2,16,2,512]{3,2,1,0:T(2,128)S(1)} %squeeze.40), channel_id=1, source_target_pairs={{2,0},{3,1},{4,2},{5,3},{6,4},{7,5},{8,6},{9,7},{10,8},{11,9},{12,... | collective-permute-start | bytes 393224 | tf_op jit(solution)/shard_map/ppermute | solution.py:16
  101.5 11.4 %collective-permute-start.9 = (f32[2,16,2,512]{3,2,1,0:T(2,128)S(1)}, f32[2,16,2,512]{3,2,1,0:T(2,128)S(1)}, u32[]{:S(2)}, u32[]{:S(2)}) collective-permute-start(f32[2,16,2,512]{3,2,1,0:T(2,128)S(1)} %squeeze.39), channel_id=1, source_target_pairs={{3,0},{4,1},{5,2},{6,3},{7,4},{8,5},{9,6},{10,7},{11,8},{12,9},{13... | collective-permute-start | bytes 393224 | tf_op jit(solution)/shard_map/ppermute | solution.py:16
  104.4 11.9 %collective-permute-start.8 = (f32[2,16,2,512]{3,2,1,0:T(2,128)S(1)}, f32[2,16,2,512]{3,2,1,0:T(2,128)S(1)}, u32[]{:S(2)}, u32[]{:S(2)}) collective-permute-start(f32[2,16,2,512]{3,2,1,0:T(2,128)S(1)} %squeeze.38), channel_id=1, source_target_pairs={{4,0},{5,1},{6,2},{7,3},{8,4},{9,5},{10,6},{11,7},{12,8},{13,9},{1... | collective-permute-start | bytes 393224 | tf_op jit(solution)/shard_map/ppermute | solution.py:16
where the time goes:
time: 118 us; the launch traced here: 117 us
  starting transfers between devices  81.2 us (69%)
  local copies, waits for them, and re-layouts  13.1 us (11%)
  matrix products  11.7 us (10%)
  waiting for transfers between devices  5.48 us (5%)
  other arithmetic  5.06 us (4%)
    ppermute x16, starting transfers between devices, passed_along(): return lax.ppermute(shard, axis, pairs)  68.4 us
    ppermute x1, starting transfers between devices, padded_2(): lax.ppermute(lax.slice_in_dim(block, 0, width, axis=dim), axis, backward)  10.2 us
    ppermute x16, waiting for transfers between devices, passed_along(): return lax.ppermute(shard, axis, pairs)  5.48 us
    dot_general x2, matrix products, shards(): lax.dot_general(masked, tables[table], (((1,), (1,)), ((), ())), preferre...  3.91 us
    slice x1, local copies, waits for them, and re-layouts, shards(): tables[table]  3.64 us
    unnamed x30, local copies, waits for them, and re-layouts  2.97 us
    ppermute x1, starting transfers between devices, padded_2(): lax.ppermute(lax.slice_in_dim(block, block.shape[dim] - width, None, axis...  2.57 us
  transfers between devices with their start and end apart: 18, of which 2 were waited for; matrix products, arithmetic and copies ran while one was open for 22% of the time, Pallas kernels for 0%

commit v1 on v0

v1 whole, which is shorter than its diff:
```python
import jax
import jax.numpy as jnp
from jax import lax
from jax.experimental import pallas as pl
from jax.experimental.pallas import tpu as pltpu
from jax.sharding import PartitionSpec as P

DELTA = 0.5
PRIOR_WEIGHT = 2.0
MESH = pl.DeviceIdType.MESH
HOPS = (-2, 2, -1, 1)
BACK = (1, 0, 3, 2)
CORES = 2
NT = (((1,), (1,)), ((), ()))


def chunks(total, width):
    return [(at, min(width, total - at)) for at in range(0, total, width)]


def kernel(
    n_grp,
    n_view,
    angle_ref,
    cover_ref,
    offset_ref,
    count_ref,
    vol_ref,
    fp_hbm,
    meas_hbm,
    out_ref,
    fp,
    meas,
    gain,
    win,
    edge,
    halo,
    sel,
    sel_t,
    hi,
    lo,
    proj,
    wres,
    gsum,
    gwin,
    from_partner,
    out_bf,
    arrived,
    load_sem,
    vol_send,
    vol_recv,
    pass_send,
    pass_recv,
    edge_send,
    edge_recv,
    pg_send,
    pg_recv,
    og_send,
    og_recv,
):
    n_dev = n_grp * n_view
    n_chip = n_dev // CORES
    me = lax.axis_index("grp") * n_view + lax.axis_index("view")
    chip = me // CORES
    core = me % CORES
    tables, plane, channels = fp.shape
    views = angle_ref.shape[0]
    slots = cover_ref.shape[0]
    rows = vol_ref.shape[0]
    slab = rows // 2
    det = meas.shape[0] // views
    chip_rows = CORES * rows
    far_rows = 2 * chip_rows
    rest_rows = 3 * chip_rows
    total_rows = tables * (far_rows + rest_rows)
    far_all = tables * far_rows

    def at(device):
        return (device // n_view, device % n_view)

    def exists(hop):
        return jnp.logical_and(chip + hop >= 0, chip + hop < n_chip)

    def peer(hop):
        return at(jnp.clip(me + CORES * hop, 0, n_dev - 1))

    partner = at(me + 1 - 2 * core)
    below, above = me - 1, me + 1
    has_below, has_above = below >= 0, above < n_dev

    loads = [pltpu.make_async_copy(fp_hbm, fp, load_sem.at[0]), pltpu.make_async_copy(meas_hbm, meas, load_sem.at[1])]
    for copy in loads:
        copy.start()

    for j, hop in enumerate(HOPS):

        @pl.when(jnp.logical_not(exists(hop)))
        def _(j=j):
            win[2 * j] = jnp.zeros_like(win[2 * j])
            win[2 * j + 1] = jnp.zeros_like(win[2 * j + 1])
            arrived[j] = jnp.zeros_like(arrived[j])

    @pl.when(jnp.logical_not(has_below))
    def _():
        halo[0] = jnp.zeros_like(halo[0])

    @pl.when(jnp.logical_not(has_above))
    def _():
        halo[1] = jnp.zeros_like(halo[1])

    win[8 + core] = vol_ref[...].astype(jnp.bfloat16)
    edge[0] = vol_ref[0:1, :]
    edge[1] = vol_ref[rows - 1 : rows, :]

    barrier = pltpu.get_barrier_semaphore()
    pl.semaphore_signal(barrier, inc=1, device_id=partner, device_id_type=MESH)
    expected = jnp.int32(1)
    for hop in HOPS:

        @pl.when(exists(hop))
        def _(hop=hop):
            pl.semaphore_signal(barrier, inc=1, device_id=peer(hop), device_id_type=MESH)

        expected = expected + exists(hop).astype(jnp.int32)
    across = jnp.where(core == 0, below, above)
    has_across = jnp.logical_and(across >= 0, across < n_dev)

    @pl.when(has_across)
    def _():
        pl.semaphore_signal(barrier, inc=1, device_id=at(across), device_id_type=MESH)

    expected = expected + has_across.astype(jnp.int32)
    pl.semaphore_wait(barrier, expected)

    vol_copies = [
        pltpu.make_async_remote_copy(
            src_ref=win.at[8 + core],
            dst_ref=win.at[2 * BACK[j] + core],
            send_sem=vol_send.at[j],
            recv_sem=vol_recv.at[BACK[j]],
            device_id=peer(hop),
            device_id_type=MESH,
        )
        for j, hop in enumerate(HOPS)
    ]
    pass_copies = [
        pltpu.make_async_remote_copy(
            src_ref=win.at[2 * j + core],
            dst_ref=win.at[2 * j + core],
            send_sem=pass_send.at[j],
            recv_sem=pass_recv.at[j],
            device_id=partner,
            device_id_type=MESH,
        )
        for j in range(5)
    ]
    edge_copies = [
        pltpu.make_async_remote_copy(
            src_ref=edge.at[side],
            dst_ref=halo.at[1 - side],
            send_sem=edge_send.at[side],
            recv_sem=edge_recv.at[1 - side],
            device_id=at(jnp.clip(target, 0, n_dev - 1)),
            device_id_type=MESH,
        )
        for side, target in enumerate((below, above))
    ]
    for j, hop in enumerate(HOPS):

        @pl.when(exists(hop))
        def _(j=j):
            vol_copies[j].start()

    pass_copies[4].start()

    @pl.when(has_below)
    def _():
        edge_copies[0].start()

    @pl.when(has_above)
    def _():
        edge_copies[1].start()

    first_block = (chip - 2) * 4
    row_of = []
    for v in range(views):
        here = []
        for k in range(slots):
            block = cover_ref[k, v] - first_block
            chip_at = block // 4
            place = 4 - 2 * jnp.abs(chip_at - 2) + jnp.where(chip_at > 2, 1, 0)
            inside = place * chip_rows + (block % 4) * slab
            table = angle_ref[v]
            row = jnp.where(
                place < 2,
                table * far_rows + inside,
                far_all + table * rest_rows + inside - far_rows,
            )
            row = row - offset_ref[k, v]
            here.append((row, offset_ref[k, v], k < count_ref[v]))
        row_of.append(here)

    det_iota = lax.broadcasted_iota(jnp.int32, (det, 128), 0)
    for v in range(views):
        goals = []
        for row, off, live in row_of[v]:
            off_live = jnp.where(live, off, -4096)
            inside = jnp.logical_and(det_iota >= off_live, det_iota < off_live + slab)
            goals.append(jnp.where(inside, det_iota + row, -1))
        for tile in range(total_rows // 128):
            lane = lax.broadcasted_iota(jnp.int32, (det, 128), 1) + tile * 128
            hits = jnp.zeros((det, 128), jnp.float32)
            for goal in goals:
                hits = hits + jnp.where(goal == lane, 1.0, 0.0)
            sel_t[pl.ds(v * det, det), pl.ds(tile * 128, 128)] = hits.astype(jnp.bfloat16)
    lane = lax.broadcasted_iota(jnp.int32, (8, views * det), 1)
    goals = []
    for k in range(slots):
        goal = jnp.full((8, views * det), -1, jnp.int32)
        for v in range(views):
            row, off, live = row_of[v][k]
            off_live = jnp.where(live, off, -4096)
            spot = lane - v * det
            inside = jnp.logical_and(
                jnp.logical_and(spot >= off_live, spot < off_live + slab),
                jnp.logical_and(spot >= 0, spot < det),
            )
            goal = jnp.where(inside, spot + row, goal)
        goals.append(goal[0:1, :])

    def build_sel(step, _):
        at_row = pl.multiple_of(step * 32, 32)
        index = lax.broadcasted_iota(jnp.int32, (32, views * det), 0) + step * 32
        hits = jnp.zeros((32, views * det), jnp.float32)
        for goal in goals:
            hits = hits + jnp.where(goal == index, 1.0, 0.0)
        sel[pl.ds(at_row, 32), :] = hits.astype(jnp.bfloat16)
        return 0

    lax.fori_loop(0, total_rows // 32, build_sel, 0)

    loads[1].wait()

    def build_gain(step, _):
        part = pl.ds(pl.multiple_of(step * 32, 32), 32)
        gain[part, :] = jnp.exp(-meas[part, :].astype(jnp.float32))
        return 0

    lax.fori_loop(0, meas.shape[0] // 32, build_gain, 0)
    loads[0].wait()

    def project(first_slot, slot_count, first_row):
        block = win[pl.ds(first_slot, slot_count)].reshape(slot_count * rows, plane)
        height = slot_count * rows
        for table in range(tables):
            for start, width in chunks(channels, 256):
                cols = pl.ds(start, width)
                product = jnp.dot(block, fp[table, :, cols], preferred_element_type=jnp.float32)
                top = product.astype(jnp.bfloat16)
                part = pl.ds(first_row + table * height, height)
                hi[part, cols] = top
                lo[part, cols] = (product - top.astype(jnp.float32)).astype(jnp.bfloat16)

    def placed(first_row, height, cols):
        pick = sel_t[:, pl.ds(first_row, height)]
        part = pl.ds(first_row, height)
        return jnp.dot(pick, hi[part, cols], preferred_element_type=jnp.float32) + jnp.dot(
            pick, lo[part, cols], preferred_element_type=jnp.float32
        )

    def collect(which):
        for j in which:

            @pl.when(exists(HOPS[j]))
            def _(j=j):
                vol_copies[BACK[j]].wait_recv()
                pass_copies[j].start()

        for j in which:

            @pl.when(exists(HOPS[j]))
            def _(j=j):
                pass_copies[j].wait_recv()

    collect((2, 3))
    pass_copies[4].wait_recv()
    project(4, 6, far_all)
    for start, width in chunks(channels, 256):
        cols = pl.ds(start, width)
        proj[:, cols] = placed(far_all, tables * rest_rows, cols)
    collect((0, 1))
    project(0, 4, 0)
    for start, width in chunks(channels, 256):
        cols = pl.ds(start, width)
        forward = proj[:, cols] + placed(0, far_all, cols)
        wres[:, cols] = (gain[:, cols] * (forward - meas[:, cols].astype(jnp.float32))).astype(jnp.bfloat16)

    def gather(first_row, height):
        part = pl.ds(first_row, height)
        for start, width in chunks(channels, 256):
            cols = pl.ds(start, width)
            gsum[part, cols] = jnp.dot(sel[part, :], wres[:, cols], preferred_element_type=jnp.float32).astype(
                jnp.bfloat16
            )

    def backproject(first_row, stride, first_slot, slot_count):
        height = slot_count * rows
        for start, width in chunks(plane, 256):
            total = None
            for table in range(tables):
                term = lax.dot_general(
                    gsum[pl.ds(first_row + table * stride, height), :],
                    fp[table, pl.ds(start, width), :],
                    NT,
                    preferred_element_type=jnp.float32,
                )
                total = term if total is None else total + term
            gwin[pl.ds(first_slot, slot_count), :, pl.ds(start, width)] = total.reshape(slot_count, rows, width)

    pg_copies = [
        pltpu.make_async_remote_copy(
            src_ref=gwin.at[2 * j + 1 - core],
            dst_ref=from_partner.at[j],
            send_sem=pg_send.at[j],
            recv_sem=pg_recv.at[j],
            device_id=partner,
            device_id_type=MESH,
        )
        for j in range(5)
    ]
    og_copies = [
        pltpu.make_async_remote_copy(
            src_ref=out_bf.at[j],
            dst_ref=arrived.at[BACK[j]],
            send_sem=og_send.at[j],
            recv_sem=og_recv.at[BACK[j]],
            device_id=peer(hop),
            device_id_type=MESH,
        )
        for j, hop in enumerate(HOPS)
    ]

    def hand_out(which):
        for j in which:
            pg_copies[j].wait_recv()
            out_bf[j] = (gwin[2 * j + core] + from_partner[j]).astype(jnp.bfloat16)

            @pl.when(exists(HOPS[j]))
            def _(j=j):
                og_copies[j].start()

    gather(0, far_all)
    backproject(0, far_rows, 0, 4)
    pg_copies[0].start()
    pg_copies[1].start()
    gather(far_all, tables * rest_rows)
    hand_out((0, 1))
    backproject(far_all, rest_rows, 4, 6)
    for j in (2, 3, 4):
        pg_copies[j].start()

    @pl.when(has_below)
    def _():
        edge_copies[1].wait_recv()

    @pl.when(has_above)
    def _():
        edge_copies[0].wait_recv()

    here = vol_ref[...]
    row = lax.broadcasted_iota(jnp.int32, here.shape, 0)
    column = lax.broadcasted_iota(jnp.int32, here.shape, 1) % (plane // 2)

    def step_to(other, allowed):
        return jnp.where(allowed, jnp.clip(here - other, -DELTA, DELTA), 0.0)

    lower = jnp.where(row == 0, halo[0], pltpu.roll(here, 1, 0))
    upper = jnp.where(row == rows - 1, halo[1], pltpu.roll(here, rows - 1, 0))
    prior = step_to(lower, row + me > 0)
    prior = prior + step_to(upper, row + (me + 1 - n_dev) < rows - 1)
    prior = prior + jnp.clip(here - pltpu.roll(here, plane // 2, 1), -DELTA, DELTA)
    prior = prior + step_to(pltpu.roll(here, 1, 1), column > 0)
    prior = prior + step_to(pltpu.roll(here, plane - 1, 1), column < plane // 2 - 1)
    out_ref[...] = PRIOR_WEIGHT * prior

    hand_out((2, 3))
    pg_copies[4].wait_recv()
    total = out_ref[...] + gwin[8 + core] + from_partner[4]
    for j in (2, 3, 0, 1):

        @pl.when(exists(HOPS[j]))
        def _(j=j):
            og_copies[BACK[j]].wait_recv()

        total = total + arrived[j].astype(jnp.float32)
    out_ref[...] = total

    for j, hop in enumerate(HOPS):

        @pl.when(exists(hop))
        def _(j=j):
            vol_copies[j].wait_send()
            pass_copies[j].wait_send()
            og_copies[j].wait_send()

    pass_copies[4].wait_send()
    for j in range(5):
        pg_copies[j].wait_send()

    @pl.when(has_below)
    def _():
        edge_copies[0].wait_send()

    @pl.when(has_above)
    def _():
        edge_copies[1].wait_send()


def solution(mesh):
    n_grp, n_view = mesh.shape["grp"], mesh.shape["view"]

    def shards(volume, footprint, measured, angle_index, cover, offset, count):
        blocks, slab, strip, width = volume.shape
        views, det, channels = measured.shape
        tables = footprint.shape[0]
        rows, plane = blocks * slab, strip * width
        total_rows = tables * 5 * CORES * rows
        bf, f32 = jnp.bfloat16, jnp.float32
        dma = pltpu.SemaphoreType.DMA
        smem = pl.BlockSpec(memory_space=pltpu.SMEM)
        vmem = pl.BlockSpec(memory_space=pltpu.VMEM)
        hbm = pl.BlockSpec(memory_space=pltpu.HBM)
        gradient = pl.pallas_call(
            lambda *refs: kernel(n_grp, n_view, *refs),
            out_shape=jax.ShapeDtypeStruct((rows, plane), f32),
            in_specs=[smem, smem, smem, smem, vmem, hbm, hbm],
            out_specs=vmem,
            scratch_shapes=[
                pltpu.VMEM((tables, plane, channels), bf),
                pltpu.VMEM((views * det, channels), bf),
                pltpu.VMEM((views * det, channels), f32),
                pltpu.VMEM((10, rows, plane), bf),
                pltpu.VMEM((2, 1, plane), f32),
                pltpu.VMEM((2, 1, plane), f32),
                pltpu.VMEM((total_rows, views * det), bf),
                pltpu.VMEM((views * det, total_rows), bf),
                pltpu.VMEM((total_rows, channels), bf),
                pltpu.VMEM((total_rows, channels), bf),
                pltpu.VMEM((views * det, channels), f32),
                pltpu.VMEM((views * det, channels), bf),
                pltpu.VMEM((total_rows, channels), bf),
                pltpu.VMEM((10, rows, plane), f32),
                pltpu.VMEM((5, rows, plane), f32),
                pltpu.VMEM((4, rows, plane), bf),
                pltpu.VMEM((4, rows, plane), bf),
                dma((2,)),
                dma((4,)),
                dma((4,)),
                dma((5,)),
                dma((5,)),
                dma((2,)),
                dma((2,)),
                dma((5,)),
                dma((5,)),
                dma((4,)),
                dma((4,)),
            ],
            compiler_params=pltpu.CompilerParams(
                collective_id=0, has_side_effects=True, vmem_limit_bytes=67_043_328
            ),
            name="ct_gradient",
        )(
            angle_index,
            cover.T,
            offset.T,
            count,
            volume.reshape(rows, plane),
            footprint.reshape(tables, plane, channels),
            measured.reshape(views * det, channels),
        )
        return gradient.reshape(volume.shape)

    axes = ("grp", "view")
    in_specs = (
        P(axes, None, None, None),
        P(axes, None, None, None),
        P(axes, None, None),
        P(axes),
        P(axes, None),
        P(axes, None),
        P(axes),
    )
    return jax.shard_map(
        shards, mesh=mesh, in_specs=in_specs, out_specs=P(axes, None, None, None), check_vma=False
    )
```

time: 118 us -> 48.5 us (0.41)
  starting transfers between devices: 81.2 us -> 0 us
  Pallas kernels: 0 us -> 45.1 us
  matrix products: 11.7 us -> 0 us
  local copies, waits for them, and re-layouts: 13.1 us -> 3.25 us
  waiting for transfers between devices: 5.48 us -> 0 us
  other arithmetic: 5.06 us -> 0 us
    ppermute x18 -> x0, starting transfers between devices: 81.2 us -> none  [the longest x16 68.4 us: passed_along(): return lax.ppermute(shard, axis, pairs)]
    pallas_call x0 -> x1, Pallas kernels: none -> 45.1 us  [shards(): pl.pallas_call(lambda *refs: kernel(n_grp, n_view, *refs), out_shape=jax....]
    dot_general x8 -> x0, matrix products: 11.7 us -> none  [the longest x2 3.91 us: shards(): lax.dot_general(masked, tables[table], (((1,), (1,)), ((), ())), preferre...]
    ppermute x18 -> x0, waiting for transfers between devices: 5.48 us -> none  [the longest x16 5.48 us: passed_along(): return lax.ppermute(shard, axis, pairs)]
    slice x3 -> x0, local copies, waits for them, and re-layouts: 4.74 us -> none  [the longest x1 3.64 us: shards(): tables[table]]
    reshape x2 -> x1, local copies, waits for them, and re-layouts: 3.47 us -> 1.67 us  [shards(): return gradient.reshape(volume.shape)]
    another operation x1 -> x0, other arithmetic: 1.49 us -> none  [shards(): jnp.stack([jnp.dot(win_rows, tables[table], preferred_element_type=jnp.fl...]
    squeeze x9 -> x0, local copies, waits for them, and re-layouts: 1.43 us -> none  [the longest x8 1.27 us: shards(): parts[REACH + step]]
  transfers between devices with their start and end apart: 18 -> 0, of which waited for: 2 -> 0; matrix products, arithmetic and copies ran while one was open for 22% -> 0% of each run, Pallas kernels for 0% -> 0%
where the time goes in v1:
time: 48.5 us; the launch traced here: 48.3 us
  Pallas kernels  45.1 us (93%)
  local copies, waits for them, and re-layouts  3.25 us (7%)
    pallas_call x1, Pallas kernels, shards(): pl.pallas_call(lambda *refs: kernel(n_grp, n_view, *refs), out_shape=jax....  45.1 us
    reshape x1, local copies, waits for them, and re-layouts, shards(): return gradient.reshape(volume.shape)  1.67 us
    unnamed x1, local copies, waits for them, and re-layouts  1.58 us

profile of v1, /device:TPU:8, one launch (start us, length us, event | category | flops | bytes accessed | tf_op | source)
XLA Modules:
  0.0 48.3 jit_solution(12491929828438410734)
XLA Ops:
  0.0 1.6 %copy.8 = f32[4,8,2,512]{3,1,2,0:T(8,128)} copy(f32[4,8,2,512]{3,2,1,0:T(2,128)} %bitcast.10) | data formatting | bytes 262144
  1.6 45.1 %ct_gradient.1 = f32[32,1024]{1,0:T(8,128)} custom-call(s32[8]{0:T(128)} %refs_0_.1, s32[4,8]{1,0:T(4,128)} %bitcast.11, s32[4,8]{1,0:T(4,128)} %bitcast.12, s32[8]{0:T(128)} %refs_3_.1, f32[32,1024]{1,0:T(8,128)} %bitcast.9, bf16[2,1024,896]{2,1,0:T(8,128)(2,1)} %bitcast.7, bf16[512,896]{1,0:T(8,128)(2,1)} %bitcast.8), custom_call_target="tpu_custom_call" | custom-call | tf_op jit(solution)/shard_map/ct_gradient/pallas_call | solution.py:433
  46.7 1.7 %reshape.15 = f32[2,16,2,512]{3,2,1,0:T(2,128)} reshape(f32[32,1024]{1,0:T(8,128)} %ct_gradient.1) | data formatting | bytes 262144 | tf_op jit(solution)/shard_map/reshape | solution.py:481

commit v2 on v1

--- a/solution.py
+++ b/solution.py
@@ -21,14 +21,20 @@
 def kernel(
     n_grp,
     n_view,
+    angle_hbm,
+    cover_hbm,
+    offset_hbm,
+    count_hbm,
+    vol_hbm,
+    fp_hbm,
+    meas_hbm,
+    out_ref,
     angle_ref,
     cover_ref,
     offset_ref,
     count_ref,
+    raw,
     vol_ref,
-    fp_hbm,
-    meas_hbm,
-    out_ref,
     fp,
     meas,
     gain,
@@ -68,6 +74,7 @@
     slots = cover_ref.shape[0]
     rows = vol_ref.shape[0]
     slab = rows // 2
+    pieces = plane // 128
     det = meas.shape[0] // views
     chip_rows = CORES * rows
     far_rows = 2 * chip_rows
@@ -88,9 +95,49 @@
     below, above = me - 1, me + 1
     has_below, has_above = below >= 0, above < n_dev
 
-    loads = [pltpu.make_async_copy(fp_hbm, fp, load_sem.at[0]), pltpu.make_async_copy(meas_hbm, meas, load_sem.at[1])]
+    barrier = pltpu.get_barrier_semaphore()
+    pl.semaphore_signal(barrier, inc=1, device_id=partner, device_id_type=MESH)
+    expected = jnp.int32(1)
+    for hop in HOPS:
+
+        @pl.when(exists(hop))
+        def _(hop=hop):
+            pl.semaphore_signal(barrier, inc=1, device_id=peer(hop), device_id_type=MESH)
+
+        expected = expected + exists(hop).astype(jnp.int32)
+    across = jnp.where(core == 0, below, above)
+    has_across = jnp.logical_and(across >= 0, across < n_dev)
+
+    @pl.when(has_across)
+    def _():
+        pl.semaphore_signal(barrier, inc=1, device_id=at(across), device_id_type=MESH)
+
+    expected = expected + has_across.astype(jnp.int32)
+
+    loads = [
+        pltpu.make_async_copy(source, target, load_sem.at[n])
+        for n, (source, target) in enumerate(
+            (
+                (vol_hbm, raw),
+                (angle_hbm, angle_ref),
+                (cover_hbm, cover_ref),
+                (offset_hbm, offset_ref),
+                (count_hbm, count_ref),
+                (meas_hbm, meas),
+                (fp_hbm, fp),
+            )
+        )
+    ]
     for copy in loads:
         copy.start()
+    loads[0].wait()
+    for piece in range(pieces):
+        at_column = ((piece % 2) * (pieces // 2) + piece // 2) * 128
+        value = raw[pl.ds(piece, rows, stride=pieces), :]
+        vol_ref[:, pl.ds(at_column, 128)] = value
+        win[8 + core, :, pl.ds(at_column, 128)] = value.astype(jnp.bfloat16)
+    edge[0] = vol_ref[0:1, :]
+    edge[1] = vol_ref[rows - 1 : rows, :]
 
     for j, hop in enumerate(HOPS):
 
@@ -108,28 +155,6 @@
     def _():
         halo[1] = jnp.zeros_like(halo[1])
 
-    win[8 + core] = vol_ref[...].astype(jnp.bfloat16)
-    edge[0] = vol_ref[0:1, :]
-    edge[1] = vol_ref[rows - 1 : rows, :]
-
-    barrier = pltpu.get_barrier_semaphore()
-    pl.semaphore_signal(barrier, inc=1, device_id=partner, device_id_type=MESH)
-    expected = jnp.int32(1)
-    for hop in HOPS:
-
-        @pl.when(exists(hop))
-        def _(hop=hop):
-            pl.semaphore_signal(barrier, inc=1, device_id=peer(hop), device_id_type=MESH)
-
-        expected = expected + exists(hop).astype(jnp.int32)
-    across = jnp.where(core == 0, below, above)
-    has_across = jnp.logical_and(across >= 0, across < n_dev)
-
-    @pl.when(has_across)
-    def _():
-        pl.semaphore_signal(barrier, inc=1, device_id=at(across), device_id_type=MESH)
-
-    expected = expected + has_across.astype(jnp.int32)
     pl.semaphore_wait(barrier, expected)
 
     vol_copies = [
@@ -165,9 +190,9 @@
         )
         for side, target in enumerate((below, above))
     ]
-    for j, hop in enumerate(HOPS):
-
-        @pl.when(exists(hop))
+    for j in (2, 3, 0, 1):
+
+        @pl.when(exists(HOPS[j]))
         def _(j=j):
             vol_copies[j].start()
 
@@ -180,6 +205,9 @@
     @pl.when(has_above)
     def _():
         edge_copies[1].start()
+
+    for copy in loads[1:5]:
+        copy.wait()
 
     first_block = (chip - 2) * 4
     row_of = []
@@ -239,7 +267,7 @@
 
     lax.fori_loop(0, total_rows // 32, build_sel, 0)
 
-    loads[1].wait()
+    loads[5].wait()
 
     def build_gain(step, _):
         part = pl.ds(pl.multiple_of(step * 32, 32), 32)
@@ -247,7 +275,7 @@
         return 0
 
     lax.fori_loop(0, meas.shape[0] // 32, build_gain, 0)
-    loads[0].wait()
+    loads[6].wait()
 
     def project(first_slot, slot_count, first_row):
         block = win[pl.ds(first_slot, slot_count)].reshape(slot_count * rows, plane)
@@ -381,11 +409,11 @@
     prior = prior + jnp.clip(here - pltpu.roll(here, plane // 2, 1), -DELTA, DELTA)
     prior = prior + step_to(pltpu.roll(here, 1, 1), column > 0)
     prior = prior + step_to(pltpu.roll(here, plane - 1, 1), column < plane // 2 - 1)
-    out_ref[...] = PRIOR_WEIGHT * prior
+    vol_ref[...] = PRIOR_WEIGHT * prior
 
     hand_out((2, 3))
     pg_copies[4].wait_recv()
-    total = out_ref[...] + gwin[8 + core] + from_partner[4]
+    total = vol_ref[...] + gwin[8 + core] + from_partner[4]
     for j in (2, 3, 0, 1):
 
         @pl.when(exists(HOPS[j]))
@@ -393,7 +421,9 @@
             og_copies[BACK[j]].wait_recv()
 
         total = total + arrived[j].astype(jnp.float32)
-    out_ref[...] = total
+    for piece in range(pieces):
+        at_column = ((piece % 2) * (pieces // 2) + piece // 2) * 128
+        out_ref[pl.ds(piece, rows, stride=pieces), :] = total[:, at_column : at_column + 128]
 
     for j, hop in enumerate(HOPS):
 
@@ -427,15 +457,20 @@
         total_rows = tables * 5 * CORES * rows
         bf, f32 = jnp.bfloat16, jnp.float32
         dma = pltpu.SemaphoreType.DMA
-        smem = pl.BlockSpec(memory_space=pltpu.SMEM)
         vmem = pl.BlockSpec(memory_space=pltpu.VMEM)
         hbm = pl.BlockSpec(memory_space=pltpu.HBM)
         gradient = pl.pallas_call(
             lambda *refs: kernel(n_grp, n_view, *refs),
-            out_shape=jax.ShapeDtypeStruct((rows, plane), f32),
-            in_specs=[smem, smem, smem, smem, vmem, hbm, hbm],
+            out_shape=jax.ShapeDtypeStruct((rows * plane // 128, 128), f32),
+            in_specs=[hbm] * 7,
             out_specs=vmem,
             scratch_shapes=[
+                pltpu.SMEM(angle_index.shape, jnp.int32),
+                pltpu.SMEM(cover.T.shape, jnp.int32),
+                pltpu.SMEM(offset.T.shape, jnp.int32),
+                pltpu.SMEM(count.shape, jnp.int32),
+                pltpu.VMEM((rows * plane // 128, 128), f32),
+                pltpu.VMEM((rows, plane), f32),
                 pltpu.VMEM((tables, plane, channels), bf),
                 pltpu.VMEM((views * det, channels), bf),
                 pltpu.VMEM((views * det, channels), f32),
@@ -453,7 +488,7 @@
                 pltpu.VMEM((5, rows, plane), f32),
                 pltpu.VMEM((4, rows, plane), bf),
                 pltpu.VMEM((4, rows, plane), bf),
-                dma((2,)),
+                dma((7,)),
                 dma((4,)),
                 dma((4,)),
                 dma((5,)),
@@ -474,11 +509,11 @@
             cover.T,
             offset.T,
             count,
-            volume.reshape(rows, plane),
+            volume.reshape(rows, strip, width // 128, 128).transpose(0, 2, 1, 3).reshape(-1, 128),
             footprint.reshape(tables, plane, channels),
             measured.reshape(views * det, channels),
         )
-        return gradient.reshape(volume.shape)
+        return gradient.reshape(rows, width // 128, strip, 128).transpose(0, 2, 1, 3).reshape(volume.shape)
 
     axes = ("grp", "view")
     in_specs = (

time: 48.5 us -> 45 us (0.928)
  Pallas kernels: 45.1 us -> 43.3 us
  local copies, waits for them, and re-layouts: 3.25 us -> 1.57 us
    pallas_call x1, Pallas kernels: 45.1 us -> 43.3 us  [shards(): pl.pallas_call(lambda *refs: kernel(n_grp, n_view, *refs), out_shape=jax....]
    reshape x1 -> x0, local copies, waits for them, and re-layouts: 1.67 us -> none  [shards(): return gradient.reshape(volume.shape)]
where the time goes in v2:
time: 45 us; the launch traced here: 44.9 us
  Pallas kernels  43.3 us (96%)
  local copies, waits for them, and re-layouts  1.57 us (3%)
    pallas_call x1, Pallas kernels, shards(): pl.pallas_call(lambda *refs: kernel(n_grp, n_view, *refs), out_shape=jax....  43.3 us
    unnamed x1, local copies, waits for them, and re-layouts  1.57 us

profile of v2, /device:TPU:8, one launch (start us, length us, event | category | flops | bytes accessed | tf_op | source)
XLA Modules:
  0.0 44.9 jit_solution(10082313629399714071)
XLA Ops:
  0.0 43.3 %ct_gradient.1 = f32[256,128]{1,0:T(8,128)} custom-call(s32[8]{0:T(128)} %refs_0_.1, s32[4,8]{1,0:T(4,128)} %bitcast.18, s32[4,8]{1,0:T(4,128)} %bitcast.19, s32[8]{0:T(128)} %refs_3_.1, f32[256,128]{1,0:T(8,128)} %bitcast.17, bf16[2,1024,896]{2,1,0:T(8,128)(2,1)} %bitcast.14, bf16[512,896]{1,0:T(8,128)(2,1)} %bitcast.15), custom_call_target="tpu_custom_call" | custom-call | tf_op jit(solution)/shard_map/ct_gradient/pallas_call | solution.py:462
  43.3 1.6 %copy.11 = f32[2,16,2,512]{3,2,1,0:T(2,128)} copy(f32[2,16,2,512]{3,2,1,0:T(2,128)} %bitcast.16) | data formatting | bytes 262144

commit v3 on v2

--- a/solution.py
+++ b/solution.py
@@ -8,9 +8,10 @@
 DELTA = 0.5
 PRIOR_WEIGHT = 2.0
 MESH = pl.DeviceIdType.MESH
-HOPS = (-2, 2, -1, 1)
-BACK = (1, 0, 3, 2)
+HOPS = (1, 2, -1, -2)
+BACK = (2, 3, 0, 1)
 CORES = 2
+LINE = 8
 NT = (((1,), (1,)), ((), ()))
 
 
@@ -49,6 +50,7 @@
     wres,
     gsum,
     gwin,
+    box,
     from_partner,
     out_bf,
     arrived,
@@ -63,6 +65,10 @@
     pg_recv,
     og_send,
     og_recv,
+    box_send,
+    box_recv,
+    fwd_send,
+    here_sem,
 ):
     n_dev = n_grp * n_view
     n_chip = n_dev // CORES
@@ -77,10 +83,13 @@
     pieces = plane // 128
     det = meas.shape[0] // views
     chip_rows = CORES * rows
-    far_rows = 2 * chip_rows
-    rest_rows = 3 * chip_rows
-    total_rows = tables * (far_rows + rest_rows)
-    far_all = tables * far_rows
+    first_rows, last_rows, hop_rows = 3 * chip_rows, 2 * chip_rows, 4 * chip_rows
+    first_all, hop_all = tables * first_rows, tables * hop_rows
+    total_rows = tables * 5 * chip_rows
+    in_line = chip % LINE
+    line = chip // LINE
+    span = CORES * LINE
+    line_below, line_above = line > 0, line < n_chip // LINE - 1
 
     def at(device):
         return (device // n_view, device % n_view)
@@ -95,24 +104,44 @@
     below, above = me - 1, me + 1
     has_below, has_above = below >= 0, above < n_dev
 
+    def crosses(hop):
+        return jnp.logical_or(in_line + hop < 0, in_line + hop >= LINE)
+
+    def direct(hop):
+        return jnp.logical_and(exists(hop), jnp.logical_not(crosses(hop))) if hop < 0 else exists(hop)
+
+    relay = jnp.logical_and(in_line < 2, line_above)
+    relay_near = jnp.logical_and(in_line == 0, line_above)
+    boxed = jnp.logical_and(in_line < 2, line_below)
+    tail = jnp.logical_and(in_line >= LINE - 2, line_above)
+    tail_last = jnp.logical_and(in_line == LINE - 1, line_above)
+
+    def device_at(offset):
+        return at(jnp.clip(me + offset, 0, n_dev - 1))
+
     barrier = pltpu.get_barrier_semaphore()
+    expected = jnp.int32(1)
+
+    def greet(allowed, offset, count=1):
+        @pl.when(allowed)
+        def _():
+            pl.semaphore_signal(barrier, inc=count, device_id=device_at(offset), device_id_type=MESH)
+
+    for hop in HOPS:
+        if hop > 0:
+            greet(jnp.logical_and(exists(hop), jnp.logical_not(crosses(hop))), CORES * hop)
+        else:
+            greet(exists(hop), CORES * hop)
+        expected = expected + direct(hop).astype(jnp.int32)
+    greet(relay, span)
+    greet(relay_near, span - CORES)
+    greet(relay, span - 2 * CORES)
+    expected = expected + boxed.astype(jnp.int32) + tail.astype(jnp.int32) + tail_last.astype(jnp.int32)
     pl.semaphore_signal(barrier, inc=1, device_id=partner, device_id_type=MESH)
-    expected = jnp.int32(1)
-    for hop in HOPS:
-
-        @pl.when(exists(hop))
-        def _(hop=hop):
-            pl.semaphore_signal(barrier, inc=1, device_id=peer(hop), device_id_type=MESH)
-
-        expected = expected + exists(hop).astype(jnp.int32)
-    across = jnp.where(core == 0, below, above)
-    has_across = jnp.logical_and(across >= 0, across < n_dev)
-
-    @pl.when(has_across)
-    def _():
-        pl.semaphore_signal(barrier, inc=1, device_id=at(across), device_id_type=MESH)
-
-    expected = expected + has_across.astype(jnp.int32)
+    greet(jnp.logical_and(core == 0, has_below), -1)
+    greet(jnp.logical_and(core == 1, jnp.logical_and(has_above, in_line < LINE - 1)), 1)
+    expected = expected + jnp.logical_and(core == 1, has_above).astype(jnp.int32)
+    expected = expected + jnp.logical_and(core == 0, in_line > 0).astype(jnp.int32)
 
     loads = [
         pltpu.make_async_copy(source, target, load_sem.at[n])
@@ -135,7 +164,7 @@
         at_column = ((piece % 2) * (pieces // 2) + piece // 2) * 128
         value = raw[pl.ds(piece, rows, stride=pieces), :]
         vol_ref[:, pl.ds(at_column, 128)] = value
-        win[8 + core, :, pl.ds(at_column, 128)] = value.astype(jnp.bfloat16)
+        win[core, :, pl.ds(at_column, 128)] = value.astype(jnp.bfloat16)
     edge[0] = vol_ref[0:1, :]
     edge[1] = vol_ref[rows - 1 : rows, :]
 
@@ -143,8 +172,8 @@
 
         @pl.when(jnp.logical_not(exists(hop)))
         def _(j=j):
-            win[2 * j] = jnp.zeros_like(win[2 * j])
-            win[2 * j + 1] = jnp.zeros_like(win[2 * j + 1])
+            win[2 + 2 * j] = jnp.zeros_like(win[2 + 2 * j])
+            win[3 + 2 * j] = jnp.zeros_like(win[3 + 2 * j])
             arrived[j] = jnp.zeros_like(arrived[j])
 
     @pl.when(jnp.logical_not(has_below))
@@ -156,11 +185,19 @@
         halo[1] = jnp.zeros_like(halo[1])
 
     pl.semaphore_wait(barrier, expected)
+
+    def say(allowed, which, offset):
+        @pl.when(allowed)
+        def _():
+            pl.semaphore_signal(here_sem.at[which], inc=1, device_id=device_at(offset), device_id_type=MESH)
+
+    say(tail_last, 0, CORES - span)
+    say(tail, 1, 2 * CORES - span)
 
     vol_copies = [
         pltpu.make_async_remote_copy(
-            src_ref=win.at[8 + core],
-            dst_ref=win.at[2 * BACK[j] + core],
+            src_ref=win.at[core],
+            dst_ref=win.at[2 + 2 * BACK[j] + core],
             send_sem=vol_send.at[j],
             recv_sem=vol_recv.at[BACK[j]],
             device_id=peer(hop),
@@ -168,16 +205,36 @@
         )
         for j, hop in enumerate(HOPS)
     ]
+    box_copy = pltpu.make_async_remote_copy(
+        src_ref=win.at[core],
+        dst_ref=box,
+        send_sem=box_send.at[0],
+        recv_sem=box_recv.at[0],
+        device_id=device_at(-span),
+        device_id_type=MESH,
+    )
+    fwd_copies = [
+        pltpu.make_async_remote_copy(
+            src_ref=box,
+            dst_ref=win.at[2 + 2 * j + core],
+            send_sem=fwd_send.at[j],
+            recv_sem=vol_recv.at[j],
+            device_id=device_at(span - CORES * (j + 1)),
+            device_id_type=MESH,
+        )
+        for j in range(2)
+    ]
+    window_slot = [2 + 2 * j for j in range(4)] + [0]
     pass_copies = [
         pltpu.make_async_remote_copy(
-            src_ref=win.at[2 * j + core],
-            dst_ref=win.at[2 * j + core],
+            src_ref=win.at[slot + core],
+            dst_ref=win.at[slot + core],
             send_sem=pass_send.at[j],
             recv_sem=pass_recv.at[j],
             device_id=partner,
             device_id_type=MESH,
         )
-        for j in range(5)
+        for j, slot in enumerate(window_slot)
     ]
     edge_copies = [
         pltpu.make_async_remote_copy(
@@ -185,20 +242,26 @@
             dst_ref=halo.at[1 - side],
             send_sem=edge_send.at[side],
             recv_sem=edge_recv.at[1 - side],
-            device_id=at(jnp.clip(target, 0, n_dev - 1)),
+            device_id=device_at(2 * side - 1),
             device_id_type=MESH,
         )
-        for side, target in enumerate((below, above))
+        for side in range(2)
     ]
-    for j in (2, 3, 0, 1):
-
-        @pl.when(exists(HOPS[j]))
+
+    @pl.when(boxed)
+    def _():
+        box_copy.start()
+
+    for j in (0, 2, 1, 3):
+
+        @pl.when(direct(HOPS[j]))
         def _(j=j):
             vol_copies[j].start()
 
     pass_copies[4].start()
-
-    @pl.when(has_below)
+    edge_waits = jnp.logical_and(core == 0, in_line == 0)
+
+    @pl.when(jnp.logical_and(has_below, jnp.logical_not(edge_waits)))
     def _():
         edge_copies[0].start()
 
@@ -215,23 +278,24 @@
         here = []
         for k in range(slots):
             block = cover_ref[k, v] - first_block
-            chip_at = block // 4
-            place = 4 - 2 * jnp.abs(chip_at - 2) + jnp.where(chip_at > 2, 1, 0)
+            distance = block // 4 - 2
+            place = jnp.where(distance >= 0, distance, 2 - distance)
             inside = place * chip_rows + (block % 4) * slab
             table = angle_ref[v]
-            row = jnp.where(
-                place < 2,
-                table * far_rows + inside,
-                far_all + table * rest_rows + inside - far_rows,
+            off = offset_ref[k, v]
+            ahead = jnp.where(
+                place < 3, table * first_rows + inside, first_all + table * last_rows + inside - first_rows
             )
-            row = row - offset_ref[k, v]
-            here.append((row, offset_ref[k, v], k < count_ref[v]))
+            behind = jnp.where(
+                place > 0, table * hop_rows + inside - chip_rows, hop_all + table * chip_rows + inside
+            )
+            here.append((ahead - off, behind - off, off, k < count_ref[v]))
         row_of.append(here)
 
     det_iota = lax.broadcasted_iota(jnp.int32, (det, 128), 0)
     for v in range(views):
         goals = []
-        for row, off, live in row_of[v]:
+        for row, _, off, live in row_of[v]:
             off_live = jnp.where(live, off, -4096)
             inside = jnp.logical_and(det_iota >= off_live, det_iota < off_live + slab)
             goals.append(jnp.where(inside, det_iota + row, -1))
@@ -246,7 +310,7 @@
     for k in range(slots):
         goal = jnp.full((8, views * det), -1, jnp.int32)
         for v in range(views):
-            row, off, live = row_of[v][k]
+            _, row, off, live = row_of[v][k]
             off_live = jnp.where(live, off, -4096)
             spot = lane - v * det
             inside = jnp.logical_and(
@@ -310,17 +374,36 @@
             def _(j=j):
                 pass_copies[j].wait_recv()
 
-    collect((2, 3))
+    @pl.when(relay)
+    def _():
+        box_copy.wait_recv()
+
+    @pl.when(relay_near)
+    def _():
+        pl.semaphore_wait(here_sem.at[0], 1)
+        fwd_copies[0].start()
+
+    @pl.when(relay)
+    def _():
+        pl.semaphore_wait(here_sem.at[1], 1)
+        fwd_copies[1].start()
+
     pass_copies[4].wait_recv()
-    project(4, 6, far_all)
+    collect((0, 1))
+    project(0, 6, 0)
     for start, width in chunks(channels, 256):
         cols = pl.ds(start, width)
-        proj[:, cols] = placed(far_all, tables * rest_rows, cols)
-    collect((0, 1))
-    project(0, 4, 0)
+        proj[:, cols] = placed(0, first_all, cols)
+    collect((2, 3))
+
+    @pl.when(jnp.logical_and(has_below, edge_waits))
+    def _():
+        edge_copies[0].start()
+
+    project(6, 4, first_all)
     for start, width in chunks(channels, 256):
         cols = pl.ds(start, width)
-        forward = proj[:, cols] + placed(0, far_all, cols)
+        forward = proj[:, cols] + placed(first_all, total_rows - first_all, cols)
         wres[:, cols] = (gain[:, cols] * (forward - meas[:, cols].astype(jnp.float32))).astype(jnp.bfloat16)
 
     def gather(first_row, height):
@@ -347,14 +430,14 @@
 
     pg_copies = [
         pltpu.make_async_remote_copy(
-            src_ref=gwin.at[2 * j + 1 - core],
+            src_ref=gwin.at[slot + 1 - core],
             dst_ref=from_partner.at[j],
             send_sem=pg_send.at[j],
             recv_sem=pg_recv.at[j],
             device_id=partner,
             device_id_type=MESH,
         )
-        for j in range(5)
+        for j, slot in enumerate(window_slot)
     ]
     og_copies = [
         pltpu.make_async_remote_copy(
@@ -371,21 +454,20 @@
     def hand_out(which):
         for j in which:
             pg_copies[j].wait_recv()
-            out_bf[j] = (gwin[2 * j + core] + from_partner[j]).astype(jnp.bfloat16)
+            out_bf[j] = (gwin[2 + 2 * j + core] + from_partner[j]).astype(jnp.bfloat16)
 
             @pl.when(exists(HOPS[j]))
             def _(j=j):
                 og_copies[j].start()
 
-    gather(0, far_all)
-    backproject(0, far_rows, 0, 4)
-    pg_copies[0].start()
-    pg_copies[1].start()
-    gather(far_all, tables * rest_rows)
-    hand_out((0, 1))
-    backproject(far_all, rest_rows, 4, 6)
-    for j in (2, 3, 4):
+    gather(0, hop_all)
+    backproject(0, hop_rows, 2, 8)
+    for j in (0, 2, 1, 3):
         pg_copies[j].start()
+    gather(hop_all, total_rows - hop_all)
+    hand_out((0, 2, 1, 3))
+    backproject(hop_all, chip_rows, 0, 2)
+    pg_copies[4].start()
 
     @pl.when(has_below)
     def _():
@@ -411,10 +493,9 @@
     prior = prior + step_to(pltpu.roll(here, plane - 1, 1), column < plane // 2 - 1)
     vol_ref[...] = PRIOR_WEIGHT * prior
 
-    hand_out((2, 3))
     pg_copies[4].wait_recv()
-    total = vol_ref[...] + gwin[8 + core] + from_partner[4]
-    for j in (2, 3, 0, 1):
+    total = vol_ref[...] + gwin[core] + from_partner[4]
+    for j in (0, 1, 2, 3):
 
         @pl.when(exists(HOPS[j]))
         def _(j=j):
@@ -427,11 +508,26 @@
 
     for j, hop in enumerate(HOPS):
 
+        @pl.when(direct(hop))
+        def _(j=j):
+            vol_copies[j].wait_send()
+
         @pl.when(exists(hop))
         def _(j=j):
-            vol_copies[j].wait_send()
             pass_copies[j].wait_send()
             og_copies[j].wait_send()
+
+    @pl.when(boxed)
+    def _():
+        box_copy.wait_send()
+
+    @pl.when(relay_near)
+    def _():
+        fwd_copies[0].wait_send()
+
+    @pl.when(relay)
+    def _():
+        fwd_copies[1].wait_send()
 
     pass_copies[4].wait_send()
     for j in range(5):
@@ -485,6 +581,7 @@
                 pltpu.VMEM((views * det, channels), bf),
                 pltpu.VMEM((total_rows, channels), bf),
                 pltpu.VMEM((10, rows, plane), f32),
+                pltpu.VMEM((rows, plane), bf),
                 pltpu.VMEM((5, rows, plane), f32),
                 pltpu.VMEM((4, rows, plane), bf),
                 pltpu.VMEM((4, rows, plane), bf),
@@ -499,6 +596,10 @@
                 dma((5,)),
                 dma((4,)),
                 dma((4,)),
+                dma((1,)),
+                dma((1,)),
+                dma((2,)),
+                pltpu.SemaphoreType.REGULAR((2,)),
             ],
             compiler_params=pltpu.CompilerParams(
                 collective_id=0, has_side_effects=True, vmem_limit_bytes=67_043_328

time: 45 us -> 40.6 us (0.902)
  the two profiles are of different devices: /device:TPU:8 before, /device:TPU:9 now
where the time goes in v3:
time: 40.6 us; the launch traced here: 40.5 us
  Pallas kernels  38.9 us (96%)
  local copies, waits for them, and re-layouts  1.57 us (4%)
    pallas_call x1, Pallas kernels, shards(): pl.pallas_call(lambda *refs: kernel(n_grp, n_view, *refs), out_shape=jax....  38.9 us
    unnamed x1, local copies, waits for them, and re-layouts  1.57 us

profile of v3, /device:TPU:9, one launch (start us, length us, event | category | flops | bytes accessed | tf_op | source)
XLA Modules:
  0.0 40.5 jit_solution(12383005843630538490)
XLA Ops:
  0.0 38.9 %ct_gradient.1 = f32[256,128]{1,0:T(8,128)} custom-call(s32[8]{0:T(128)} %refs_0_.1, s32[4,8]{1,0:T(4,128)} %bitcast.18, s32[4,8]{1,0:T(4,128)} %bitcast.19, s32[8]{0:T(128)} %refs_3_.1, f32[256,128]{1,0:T(8,128)} %bitcast.17, bf16[2,1024,896]{2,1,0:T(8,128)(2,1)} %bitcast.14, bf16[512,896]{1,0:T(8,128)(2,1)} %bitcast.15), custom_call_target="tpu_custom_call" | custom-call | tf_op jit(solution)/shard_map/ct_gradient/pallas_call | solution.py:558
  38.9 1.6 %copy.11 = f32[2,16,2,512]{3,2,1,0:T(2,128)} copy(f32[2,16,2,512]{3,2,1,0:T(2,128)} %bitcast.16) | data formatting | bytes 262144

commit v4 on v3

--- a/solution.py
+++ b/solution.py
@@ -8,8 +8,9 @@
 DELTA = 0.5
 PRIOR_WEIGHT = 2.0
 MESH = pl.DeviceIdType.MESH
-HOPS = (1, 2, -1, -2)
-BACK = (2, 3, 0, 1)
+HOPS = (1, -1, 2, -2)
+BACK = (1, 0, 3, 2)
+GRAD_SLOT = (0, 4, 2, 6, 8)
 CORES = 2
 LINE = 8
 NT = (((1,), (1,)), ((), ()))
@@ -29,7 +30,8 @@
     vol_hbm,
     fp_hbm,
     meas_hbm,
-    out_ref,
+    out_hbm,
+    prior_hbm,
     angle_ref,
     cover_ref,
     offset_ref,
@@ -69,6 +71,9 @@
     box_recv,
     fwd_send,
     here_sem,
+    out_ref,
+    prior_ref,
+    store_sem,
 ):
     n_dev = n_grp * n_view
     n_chip = n_dev // CORES
@@ -83,8 +88,9 @@
     pieces = plane // 128
     det = meas.shape[0] // views
     chip_rows = CORES * rows
-    first_rows, last_rows, hop_rows = 3 * chip_rows, 2 * chip_rows, 4 * chip_rows
-    first_all, hop_all = tables * first_rows, tables * hop_rows
+    first_rows, last_rows = 3 * chip_rows, 2 * chip_rows
+    first_all = tables * first_rows
+    side_all = tables * last_rows
     total_rows = tables * 5 * chip_rows
     in_line = chip % LINE
     line = chip // LINE
@@ -111,10 +117,9 @@
         return jnp.logical_and(exists(hop), jnp.logical_not(crosses(hop))) if hop < 0 else exists(hop)
 
     relay = jnp.logical_and(in_line < 2, line_above)
-    relay_near = jnp.logical_and(in_line == 0, line_above)
     boxed = jnp.logical_and(in_line < 2, line_below)
-    tail = jnp.logical_and(in_line >= LINE - 2, line_above)
-    tail_last = jnp.logical_and(in_line == LINE - 1, line_above)
+    tail = jnp.logical_and(in_line == LINE - 1, line_above)
+    to_tail = span - CORES * (1 + in_line)
 
     def device_at(offset):
         return at(jnp.clip(me + offset, 0, n_dev - 1))
@@ -134,9 +139,8 @@
             greet(exists(hop), CORES * hop)
         expected = expected + direct(hop).astype(jnp.int32)
     greet(relay, span)
-    greet(relay_near, span - CORES)
-    greet(relay, span - 2 * CORES)
-    expected = expected + boxed.astype(jnp.int32) + tail.astype(jnp.int32) + tail_last.astype(jnp.int32)
+    greet(relay, to_tail)
+    expected = expected + boxed.astype(jnp.int32) + 2 * tail.astype(jnp.int32)
     pl.semaphore_signal(barrier, inc=1, device_id=partner, device_id_type=MESH)
     greet(jnp.logical_and(core == 0, has_below), -1)
     greet(jnp.logical_and(core == 1, jnp.logical_and(has_above, in_line < LINE - 1)), 1)
@@ -159,6 +163,14 @@
     ]
     for copy in loads:
         copy.start()
+    pl.semaphore_wait(barrier, expected)
+
+    for offset in (CORES - span, 2 * CORES - span):
+
+        @pl.when(tail)
+        def _(offset=offset):
+            pl.semaphore_signal(here_sem.at[0], inc=1, device_id=device_at(offset), device_id_type=MESH)
+
     loads[0].wait()
     for piece in range(pieces):
         at_column = ((piece % 2) * (pieces // 2) + piece // 2) * 128
@@ -184,15 +196,6 @@
     def _():
         halo[1] = jnp.zeros_like(halo[1])
 
-    pl.semaphore_wait(barrier, expected)
-
-    def say(allowed, which, offset):
-        @pl.when(allowed)
-        def _():
-            pl.semaphore_signal(here_sem.at[which], inc=1, device_id=device_at(offset), device_id_type=MESH)
-
-    say(tail_last, 0, CORES - span)
-    say(tail, 1, 2 * CORES - span)
 
     vol_copies = [
         pltpu.make_async_remote_copy(
@@ -213,17 +216,22 @@
         device_id=device_at(-span),
         device_id_type=MESH,
     )
-    fwd_copies = [
-        pltpu.make_async_remote_copy(
-            src_ref=box,
-            dst_ref=win.at[2 + 2 * j + core],
-            send_sem=fwd_send.at[j],
-            recv_sem=vol_recv.at[j],
-            device_id=device_at(span - CORES * (j + 1)),
-            device_id_type=MESH,
-        )
-        for j in range(2)
-    ]
+    fwd_copy = pltpu.make_async_remote_copy(
+        src_ref=box,
+        dst_ref=win.at[2 + 4 * in_line + core],
+        send_sem=fwd_send.at[0],
+        recv_sem=vol_recv.at[2 * in_line],
+        device_id=device_at(to_tail),
+        device_id_type=MESH,
+    )
+    step_copy = pltpu.make_async_remote_copy(
+        src_ref=win.at[2 + core],
+        dst_ref=win.at[6 + core],
+        send_sem=fwd_send.at[1],
+        recv_sem=vol_recv.at[2],
+        device_id=device_at(-CORES),
+        device_id_type=MESH,
+    )
     window_slot = [2 + 2 * j for j in range(4)] + [0]
     pass_copies = [
         pltpu.make_async_remote_copy(
@@ -252,7 +260,7 @@
     def _():
         box_copy.start()
 
-    for j in (0, 2, 1, 3):
+    for j in range(4):
 
         @pl.when(direct(HOPS[j]))
         def _(j=j):
@@ -279,16 +287,17 @@
         for k in range(slots):
             block = cover_ref[k, v] - first_block
             distance = block // 4 - 2
-            place = jnp.where(distance >= 0, distance, 2 - distance)
-            inside = place * chip_rows + (block % 4) * slab
+            reach = jnp.abs(distance)
+            within = (block % 4) * slab
             table = angle_ref[v]
             off = offset_ref[k, v]
+            under = jnp.where(distance < 0, 1, 0)
+            place = jnp.where(reach == 0, 0, 2 * reach - 1 + under) * chip_rows + within
             ahead = jnp.where(
-                place < 3, table * first_rows + inside, first_all + table * last_rows + inside - first_rows
+                reach < 2, table * first_rows + place, first_all + table * last_rows + place - first_rows
             )
-            behind = jnp.where(
-                place > 0, table * hop_rows + inside - chip_rows, hop_all + table * chip_rows + inside
-            )
+            side = under * side_all + table * last_rows + (reach - 1) * chip_rows + within
+            behind = jnp.where(reach > 0, side, 2 * side_all + table * chip_rows + within)
             here.append((ahead - off, behind - off, off, k < count_ref[v]))
         row_of.append(here)
 
@@ -368,6 +377,12 @@
                 vol_copies[BACK[j]].wait_recv()
                 pass_copies[j].start()
 
+            if j == 0:
+
+                @pl.when(tail)
+                def _():
+                    step_copy.start()
+
         for j in which:
 
             @pl.when(exists(HOPS[j]))
@@ -377,33 +392,25 @@
     @pl.when(relay)
     def _():
         box_copy.wait_recv()
-
-    @pl.when(relay_near)
-    def _():
         pl.semaphore_wait(here_sem.at[0], 1)
-        fwd_copies[0].start()
-
-    @pl.when(relay)
-    def _():
-        pl.semaphore_wait(here_sem.at[1], 1)
-        fwd_copies[1].start()
+        fwd_copy.start()
 
     pass_copies[4].wait_recv()
     collect((0, 1))
+
+    @pl.when(jnp.logical_and(has_below, edge_waits))
+    def _():
+        edge_copies[0].start()
+
     project(0, 6, 0)
     for start, width in chunks(channels, 256):
         cols = pl.ds(start, width)
         proj[:, cols] = placed(0, first_all, cols)
     collect((2, 3))
-
-    @pl.when(jnp.logical_and(has_below, edge_waits))
-    def _():
-        edge_copies[0].start()
-
     project(6, 4, first_all)
     for start, width in chunks(channels, 256):
         cols = pl.ds(start, width)
-        forward = proj[:, cols] + placed(first_all, total_rows - first_all, cols)
+        forward = proj[:, cols] + placed(first_all, side_all, cols)
         wres[:, cols] = (gain[:, cols] * (forward - meas[:, cols].astype(jnp.float32))).astype(jnp.bfloat16)
 
     def gather(first_row, height):
@@ -430,14 +437,14 @@
 
     pg_copies = [
         pltpu.make_async_remote_copy(
-            src_ref=gwin.at[slot + 1 - core],
+            src_ref=gwin.at[GRAD_SLOT[j] + 1 - core],
             dst_ref=from_partner.at[j],
             send_sem=pg_send.at[j],
             recv_sem=pg_recv.at[j],
             device_id=partner,
             device_id_type=MESH,
         )
-        for j, slot in enumerate(window_slot)
+        for j in range(5)
     ]
     og_copies = [
         pltpu.make_async_remote_copy(
@@ -454,19 +461,24 @@
     def hand_out(which):
         for j in which:
             pg_copies[j].wait_recv()
-            out_bf[j] = (gwin[2 + 2 * j + core] + from_partner[j]).astype(jnp.bfloat16)
+            out_bf[j] = (gwin[GRAD_SLOT[j] + core] + from_partner[j]).astype(jnp.bfloat16)
 
             @pl.when(exists(HOPS[j]))
             def _(j=j):
                 og_copies[j].start()
 
-    gather(0, hop_all)
-    backproject(0, hop_rows, 2, 8)
-    for j in (0, 2, 1, 3):
-        pg_copies[j].start()
-    gather(hop_all, total_rows - hop_all)
-    hand_out((0, 2, 1, 3))
-    backproject(hop_all, chip_rows, 0, 2)
+    gather(0, side_all)
+    backproject(0, last_rows, 0, 4)
+    pg_copies[0].start()
+    pg_copies[2].start()
+    gather(side_all, side_all)
+    hand_out((0, 2))
+    backproject(side_all, last_rows, 4, 4)
+    pg_copies[1].start()
+    pg_copies[3].start()
+    gather(2 * side_all, tables * chip_rows)
+    hand_out((1, 3))
+    backproject(2 * side_all, chip_rows, 8, 2)
     pg_copies[4].start()
 
     @pl.when(has_below)
@@ -491,11 +503,16 @@
     prior = prior + jnp.clip(here - pltpu.roll(here, plane // 2, 1), -DELTA, DELTA)
     prior = prior + step_to(pltpu.roll(here, 1, 1), column > 0)
     prior = prior + step_to(pltpu.roll(here, plane - 1, 1), column < plane // 2 - 1)
-    vol_ref[...] = PRIOR_WEIGHT * prior
+    prior = PRIOR_WEIGHT * prior
+    for piece in range(pieces):
+        at_column = ((piece % 2) * (pieces // 2) + piece // 2) * 128
+        prior_ref[pl.ds(piece, rows, stride=pieces), :] = prior[:, at_column : at_column + 128]
+    prior_store = pltpu.make_async_copy(prior_ref, prior_hbm, store_sem.at[0])
+    prior_store.start()
 
     pg_copies[4].wait_recv()
-    total = vol_ref[...] + gwin[core] + from_partner[4]
-    for j in (0, 1, 2, 3):
+    total = gwin[8 + core] + from_partner[4]
+    for j in range(4):
 
         @pl.when(exists(HOPS[j]))
         def _(j=j):
@@ -505,6 +522,8 @@
     for piece in range(pieces):
         at_column = ((piece % 2) * (pieces // 2) + piece // 2) * 128
         out_ref[pl.ds(piece, rows, stride=pieces), :] = total[:, at_column : at_column + 128]
+    out_store = pltpu.make_async_copy(out_ref, out_hbm, store_sem.at[1])
+    out_store.start()
 
     for j, hop in enumerate(HOPS):
 
@@ -521,13 +540,13 @@
     def _():
         box_copy.wait_send()
 
-    @pl.when(relay_near)
-    def _():
-        fwd_copies[0].wait_send()
-
     @pl.when(relay)
     def _():
-        fwd_copies[1].wait_send()
+        fwd_copy.wait_send()
+
+    @pl.when(tail)
+    def _():
+        step_copy.wait_send()
 
     pass_copies[4].wait_send()
     for j in range(5):
@@ -540,6 +559,9 @@
     @pl.when(has_above)
     def _():
         edge_copies[1].wait_send()
+
+    prior_store.wait()
+    out_store.wait()
 
 
 def solution(mesh):
@@ -553,13 +575,12 @@
         total_rows = tables * 5 * CORES * rows
         bf, f32 = jnp.bfloat16, jnp.float32
         dma = pltpu.SemaphoreType.DMA
-        vmem = pl.BlockSpec(memory_space=pltpu.VMEM)
         hbm = pl.BlockSpec(memory_space=pltpu.HBM)
-        gradient = pl.pallas_call(
+        data, prior = pl.pallas_call(
             lambda *refs: kernel(n_grp, n_view, *refs),
-            out_shape=jax.ShapeDtypeStruct((rows * plane // 128, 128), f32),
+            out_shape=[jax.ShapeDtypeStruct((rows * plane // 128, 128), f32)] * 2,
             in_specs=[hbm] * 7,
-            out_specs=vmem,
+            out_specs=[hbm, hbm],
             scratch_shapes=[
                 pltpu.SMEM(angle_index.shape, jnp.int32),
                 pltpu.SMEM(cover.T.shape, jnp.int32),
@@ -599,7 +620,10 @@
                 dma((1,)),
                 dma((1,)),
                 dma((2,)),
-                pltpu.SemaphoreType.REGULAR((2,)),
+                pltpu.SemaphoreType.REGULAR((1,)),
+                pltpu.VMEM((rows * plane // 128, 128), f32),
+                pltpu.VMEM((rows * plane // 128, 128), f32),
+                dma((2,)),
             ],
             compiler_params=pltpu.CompilerParams(
                 collective_id=0, has_side_effects=True, vmem_limit_bytes=67_043_328
@@ -614,6 +638,7 @@
             footprint.reshape(tables, plane, channels),
             measured.reshape(views * det, channels),
         )
+        gradient = data + prior
         return gradient.reshape(rows, width // 128, strip, 128).transpose(0, 2, 1, 3).reshape(volume.shape)
 
     axes = ("grp", "view")

time: 40.6 us -> 39 us (0.961)
  the two profiles are of different devices: /device:TPU:9 before, /device:TPU:73 now
where the time goes in v4:
time: 39 us; the launch traced here: 38.9 us
  Pallas kernels  37.3 us (96%)
  other arithmetic  1.64 us (4%)
    pallas_call x1, Pallas kernels, shards(): pl.pallas_call(lambda *refs: kernel(n_grp, n_view, *refs), out_shape=[jax...  37.3 us
    add x1, other arithmetic, shards(): gradient = data + prior  1.64 us

profile of v4, /device:TPU:73, one launch (start us, length us, event | category | flops | bytes accessed | tf_op | source)
XLA Modules:
  0.0 38.9 jit_solution(11142106127411263188)
XLA Ops:
  0.0 37.3 %ct_gradient.1 = (f32[256,128]{1,0:T(8,128)}, f32[256,128]{1,0:T(8,128)}) custom-call(s32[8]{0:T(128)} %refs_0_.1, s32[4,8]{1,0:T(4,128)} %bitcast.17, s32[4,8]{1,0:T(4,128)} %bitcast.18, s32[8]{0:T(128)} %refs_3_.1, f32[256,128]{1,0:T(8,128)} %bitcast.16, bf16[2,1024,896]{2,1,0:T(8,128)(2,1)} %bitcast.14, bf16[512,896]{1,0:T(8,128)(2,1)} %bitcast.15), custom_call_target="tpu_custom_call" | custom-call | tf_op jit(solution)/shard_map/ct_gradient/pallas_call | solution.py:579
  37.3 1.6 %add.3 = f32[256,128]{1,0:T(8,128)} add(f32[256,128]{1,0:T(8,128)} %get-tuple-element.7, f32[256,128]{1,0:T(8,128)} %get-tuple-element.8) | non-fusion elementwise | flops 32768 | bytes 393216 | tf_op jit(solution)/shard_map/add | solution.py:641

commit v5 on v4

--- a/solution.py
+++ b/solution.py
@@ -30,8 +30,8 @@
     vol_hbm,
     fp_hbm,
     meas_hbm,
-    out_hbm,
-    prior_hbm,
+    out_ref,
+    prior_ref,
     angle_ref,
     cover_ref,
     offset_ref,
@@ -71,9 +71,6 @@
     box_recv,
     fwd_send,
     here_sem,
-    out_ref,
-    prior_ref,
-    store_sem,
 ):
     n_dev = n_grp * n_view
     n_chip = n_dev // CORES
@@ -507,8 +504,6 @@
     for piece in range(pieces):
         at_column = ((piece % 2) * (pieces // 2) + piece // 2) * 128
         prior_ref[pl.ds(piece, rows, stride=pieces), :] = prior[:, at_column : at_column + 128]
-    prior_store = pltpu.make_async_copy(prior_ref, prior_hbm, store_sem.at[0])
-    prior_store.start()
 
     pg_copies[4].wait_recv()
     total = gwin[8 + core] + from_partner[4]
@@ -522,8 +517,6 @@
     for piece in range(pieces):
         at_column = ((piece % 2) * (pieces // 2) + piece // 2) * 128
         out_ref[pl.ds(piece, rows, stride=pieces), :] = total[:, at_column : at_column + 128]
-    out_store = pltpu.make_async_copy(out_ref, out_hbm, store_sem.at[1])
-    out_store.start()
 
     for j, hop in enumerate(HOPS):
 
@@ -559,9 +552,6 @@
     @pl.when(has_above)
     def _():
         edge_copies[1].wait_send()
-
-    prior_store.wait()
-    out_store.wait()
 
 
 def solution(mesh):
@@ -580,7 +570,7 @@
             lambda *refs: kernel(n_grp, n_view, *refs),
             out_shape=[jax.ShapeDtypeStruct((rows * plane // 128, 128), f32)] * 2,
             in_specs=[hbm] * 7,
-            out_specs=[hbm, hbm],
+            out_specs=[pl.BlockSpec(memory_space=pltpu.VMEM)] * 2,
             scratch_shapes=[
                 pltpu.SMEM(angle_index.shape, jnp.int32),
                 pltpu.SMEM(cover.T.shape, jnp.int32),
@@ -621,22 +611,24 @@
                 dma((1,)),
                 dma((2,)),
                 pltpu.SemaphoreType.REGULAR((1,)),
-                pltpu.VMEM((rows * plane // 128, 128), f32),
-                pltpu.VMEM((rows * plane // 128, 128), f32),
-                dma((2,)),
             ],
             compiler_params=pltpu.CompilerParams(
-                collective_id=0, has_side_effects=True, vmem_limit_bytes=67_043_328
+                collective_id=0, has_side_effects=True, vmem_limit_bytes=48 * 1024 * 1024
             ),
             name="ct_gradient",
         )(
-            angle_index,
-            cover.T,
-            offset.T,
-            count,
-            volume.reshape(rows, strip, width // 128, 128).transpose(0, 2, 1, 3).reshape(-1, 128),
-            footprint.reshape(tables, plane, channels),
-            measured.reshape(views * det, channels),
+            *(
+                pltpu.with_memory_space_constraint(array, pltpu.HBM)
+                for array in (
+                    angle_index,
+                    cover.T,
+                    offset.T,
+                    count,
+                    volume.reshape(rows, strip, width // 128, 128).transpose(0, 2, 1, 3).reshape(-1, 128),
+                    footprint.reshape(tables, plane, channels),
+                    measured.reshape(views * det, channels),
+                )
+            )
         )
         gradient = data + prior
         return gradient.reshape(rows, width // 128, strip, 128).transpose(0, 2, 1, 3).reshape(volume.shape)

time: 39 us -> 37.4 us (0.959)
  other arithmetic: 1.64 us -> 0.67 us
  Pallas kernels: 37.3 us -> 36.6 us
    add x1, other arithmetic: 1.64 us -> 0.67 us  [shards(): gradient = data + prior]
    pallas_call x1, Pallas kernels: 37.3 us -> 36.6 us  [shards(): pl.pallas_call(lambda *refs: kernel(n_grp, n_view, *refs), out_shape=[jax...]
where the time goes in v5:
time: 37.4 us; the launch traced here: 37.3 us
  Pallas kernels  36.6 us (98%)
  other arithmetic  0.67 us (2%)
    pallas_call x1, Pallas kernels, shards(): pl.pallas_call(lambda *refs: kernel(n_grp, n_view, *refs), out_shape=[jax...  36.6 us

profile of v5, /device:TPU:73, one launch (start us, length us, event | category | flops | bytes accessed | tf_op | source)
XLA Modules:
  0.0 37.3 jit_solution(16699461326196866364)
XLA Ops:
  0.0 36.6 %ct_gradient.1 = (f32[256,128]{1,0:T(8,128)S(1)}, f32[256,128]{1,0:T(8,128)S(1)}) custom-call(s32[8]{0:T(128)} %refs_0_.1, s32[4,8]{1,0:T(4,128)} %bitcast.17, s32[4,8]{1,0:T(4,128)} %bitcast.18, s32[8]{0:T(128)} %refs_3_.1, f32[256,128]{1,0:T(8,128)} %bitcast.16, bf16[2,1024,896]{2,1,0:T(8,128)(2,1)} %bitcast.14, bf16[512,896]{1,0:T(8,128)(2,1)} %bitcast.15), custom_call_target="tpu_custom_call" | custom-call | tf_op jit(solution)/shard_map/ct_gradient/pallas_call | solution.py:569
  36.6 0.7 %add.3 = f32[256,128]{1,0:T(8,128)} add(f32[256,128]{1,0:T(8,128)S(1)} %get-tuple-element.7, f32[256,128]{1,0:T(8,128)S(1)} %get-tuple-element.8) | non-fusion elementwise | flops 32768 | bytes 393216 | tf_op jit(solution)/shard_map/add | solution.py:633

commit v6 on v5

--- a/solution.py
+++ b/solution.py
@@ -47,7 +47,6 @@
     sel,
     sel_t,
     hi,
-    lo,
     proj,
     wres,
     gsum,
@@ -71,6 +70,11 @@
     box_recv,
     fwd_send,
     here_sem,
+    gbox,
+    gbox_send,
+    gbox_recv,
+    gfwd_send,
+    gfwd_recv,
 ):
     n_dev = n_grp * n_view
     n_chip = n_dev // CORES
@@ -121,6 +125,23 @@
     def device_at(offset):
         return at(jnp.clip(me + offset, 0, n_dev - 1))
 
+    loads = [
+        pltpu.make_async_copy(source, target, load_sem.at[n])
+        for n, (source, target) in enumerate(
+            (
+                (vol_hbm, raw),
+                (angle_hbm, angle_ref),
+                (cover_hbm, cover_ref),
+                (offset_hbm, offset_ref),
+                (count_hbm, count_ref),
+                (meas_hbm, meas),
+                (fp_hbm, fp),
+            )
+        )
+    ]
+    for copy in loads[:5]:
+        copy.start()
+
     barrier = pltpu.get_barrier_semaphore()
     expected = jnp.int32(1)
 
@@ -144,22 +165,6 @@
     expected = expected + jnp.logical_and(core == 1, has_above).astype(jnp.int32)
     expected = expected + jnp.logical_and(core == 0, in_line > 0).astype(jnp.int32)
 
-    loads = [
-        pltpu.make_async_copy(source, target, load_sem.at[n])
-        for n, (source, target) in enumerate(
-            (
-                (vol_hbm, raw),
-                (angle_hbm, angle_ref),
-                (cover_hbm, cover_ref),
-                (offset_hbm, offset_ref),
-                (count_hbm, count_ref),
-                (meas_hbm, meas),
-                (fp_hbm, fp),
-            )
-        )
-    ]
-    for copy in loads:
-        copy.start()
     pl.semaphore_wait(barrier, expected)
 
     for offset in (CORES - span, 2 * CORES - span):
@@ -169,6 +174,8 @@
             pl.semaphore_signal(here_sem.at[0], inc=1, device_id=device_at(offset), device_id_type=MESH)
 
     loads[0].wait()
+    for copy in loads[5:]:
+        copy.start()
     for piece in range(pieces):
         at_column = ((piece % 2) * (pieces // 2) + piece // 2) * 128
         value = raw[pl.ds(piece, rows, stride=pieces), :]
@@ -354,17 +361,12 @@
             for start, width in chunks(channels, 256):
                 cols = pl.ds(start, width)
                 product = jnp.dot(block, fp[table, :, cols], preferred_element_type=jnp.float32)
-                top = product.astype(jnp.bfloat16)
-                part = pl.ds(first_row + table * height, height)
-                hi[part, cols] = top
-                lo[part, cols] = (product - top.astype(jnp.float32)).astype(jnp.bfloat16)
+                hi[pl.ds(first_row + table * height, height), cols] = product.astype(jnp.bfloat16)
 
     def placed(first_row, height, cols):
         pick = sel_t[:, pl.ds(first_row, height)]
         part = pl.ds(first_row, height)
-        return jnp.dot(pick, hi[part, cols], preferred_element_type=jnp.float32) + jnp.dot(
-            pick, lo[part, cols], preferred_element_type=jnp.float32
-        )
+        return jnp.dot(pick, hi[part, cols], preferred_element_type=jnp.float32)
 
     def collect(which):
         for j in which:
@@ -455,14 +457,53 @@
         for j, hop in enumerate(HOPS)
     ]
 
+    half = rows // 2
+    og_half = pltpu.make_async_remote_copy(
+        src_ref=out_bf.at[2, pl.ds(0, half)],
+        dst_ref=arrived.at[3, pl.ds(0, half)],
+        send_sem=og_send.at[2],
+        recv_sem=og_recv.at[3],
+        device_id=peer(HOPS[2]),
+        device_id_type=MESH,
+    )
+    gbox_copy = pltpu.make_async_remote_copy(
+        src_ref=out_bf.at[2, pl.ds(half, half)],
+        dst_ref=gbox,
+        send_sem=gbox_send.at[0],
+        recv_sem=gbox_recv.at[0],
+        device_id=device_at(2 * CORES - span),
+        device_id_type=MESH,
+    )
+    gfwd_copy = pltpu.make_async_remote_copy(
+        src_ref=gbox,
+        dst_ref=arrived.at[3, pl.ds(half, half)],
+        send_sem=gfwd_send.at[0],
+        recv_sem=gfwd_recv.at[0],
+        device_id=device_at(span),
+        device_id_type=MESH,
+    )
+    second = in_line == 1
+    gives_half = jnp.logical_and(second, line_above)
+    takes_half = jnp.logical_and(second, line_below)
+
+    def whole(j):
+        return jnp.logical_and(exists(HOPS[j]), jnp.logical_not(tail)) if j == 2 else exists(HOPS[j])
+
     def hand_out(which):
         for j in which:
             pg_copies[j].wait_recv()
             out_bf[j] = (gwin[GRAD_SLOT[j] + core] + from_partner[j]).astype(jnp.bfloat16)
 
-            @pl.when(exists(HOPS[j]))
+            @pl.when(whole(j))
             def _(j=j):
                 og_copies[j].start()
+
+            if j == 2:
+
+                @pl.when(tail)
+                def _():
+                    gbox_copy.start()
+                    og_half.start()
 
     gather(0, side_all)
     backproject(0, last_rows, 0, 4)
@@ -505,11 +546,25 @@
         at_column = ((piece % 2) * (pieces // 2) + piece // 2) * 128
         prior_ref[pl.ds(piece, rows, stride=pieces), :] = prior[:, at_column : at_column + 128]
 
+    @pl.when(gives_half)
+    def _():
+        gbox_copy.wait_recv()
+        gfwd_copy.start()
+
     pg_copies[4].wait_recv()
     total = gwin[8 + core] + from_partner[4]
     for j in range(4):
 
-        @pl.when(exists(HOPS[j]))
+        comes = exists(HOPS[j])
+        if j == 3:
+            comes = jnp.logical_and(comes, jnp.logical_not(takes_half))
+
+            @pl.when(takes_half)
+            def _():
+                og_half.wait_recv()
+                gfwd_copy.wait_recv()
+
+        @pl.when(comes)
         def _(j=j):
             og_copies[BACK[j]].wait_recv()
 
@@ -527,7 +582,19 @@
         @pl.when(exists(hop))
         def _(j=j):
             pass_copies[j].wait_send()
+
+        @pl.when(whole(j))
+        def _(j=j):
             og_copies[j].wait_send()
+
+    @pl.when(tail)
+    def _():
+        og_half.wait_send()
+        gbox_copy.wait_send()
+
+    @pl.when(gives_half)
+    def _():
+        gfwd_copy.wait_send()
 
     @pl.when(boxed)
     def _():
@@ -587,7 +654,6 @@
                 pltpu.VMEM((total_rows, views * det), bf),
                 pltpu.VMEM((views * det, total_rows), bf),
                 pltpu.VMEM((total_rows, channels), bf),
-                pltpu.VMEM((total_rows, channels), bf),
                 pltpu.VMEM((views * det, channels), f32),
                 pltpu.VMEM((views * det, channels), bf),
                 pltpu.VMEM((total_rows, channels), bf),
@@ -611,6 +677,11 @@
                 dma((1,)),
                 dma((2,)),
                 pltpu.SemaphoreType.REGULAR((1,)),
+                pltpu.VMEM((rows // 2, plane), bf),
+                dma((1,)),
+                dma((1,)),
+                dma((1,)),
+                dma((1,)),
             ],
             compiler_params=pltpu.CompilerParams(
                 collective_id=0, has_side_effects=True, vmem_limit_bytes=48 * 1024 * 1024

time: 37.4 us -> 35.7 us (0.955)
  the two profiles are of different devices: /device:TPU:73 before, /device:TPU:8 now
where the time goes in v6:
time: 35.7 us; the launch traced here: 35.2 us
  Pallas kernels  34.6 us (97%)
  other arithmetic  0.67 us (2%)
    pallas_call x1, Pallas kernels, shards(): pl.pallas_call(lambda *refs: kernel(n_grp, n_view, *refs), out_shape=[jax...  34.6 us

profile of v6, /device:TPU:8, one launch (start us, length us, event | category | flops | bytes accessed | tf_op | source)
XLA Modules:
  0.0 35.2 jit_solution(6996394393020283671)
XLA Ops:
  0.0 34.6 %ct_gradient.1 = (f32[256,128]{1,0:T(8,128)S(1)}, f32[256,128]{1,0:T(8,128)S(1)}) custom-call(s32[8]{0:T(128)} %refs_0_.1, s32[4,8]{1,0:T(4,128)} %bitcast.17, s32[4,8]{1,0:T(4,128)} %bitcast.18, s32[8]{0:T(128)} %refs_3_.1, f32[256,128]{1,0:T(8,128)} %bitcast.16, bf16[2,1024,896]{2,1,0:T(8,128)(2,1)} %bitcast.14, bf16[512,896]{1,0:T(8,128)(2,1)} %bitcast.15), custom_call_target="tpu_custom_call" | custom-call | tf_op jit(solution)/shard_map/ct_gradient/pallas_call | solution.py:636
  34.6 0.7 %add.3 = f32[256,128]{1,0:T(8,128)} add(f32[256,128]{1,0:T(8,128)S(1)} %get-tuple-element.7, f32[256,128]{1,0:T(8,128)S(1)} %get-tuple-element.8) | non-fusion elementwise | flops 32768 | bytes 393216 | tf_op jit(solution)/shard_map/add | solution.py:704

commit v7 on v6

--- a/solution.py
+++ b/solution.py
@@ -70,6 +70,7 @@
     box_recv,
     fwd_send,
     here_sem,
+    up_sem,
     gbox,
     gbox_send,
     gbox_recv,
@@ -151,20 +152,14 @@
             pl.semaphore_signal(barrier, inc=count, device_id=device_at(offset), device_id_type=MESH)
 
     for hop in HOPS:
-        if hop > 0:
-            greet(jnp.logical_and(exists(hop), jnp.logical_not(crosses(hop))), CORES * hop)
-        else:
-            greet(exists(hop), CORES * hop)
-        expected = expected + direct(hop).astype(jnp.int32)
+        inside = jnp.logical_and(exists(hop), jnp.logical_not(crosses(hop)))
+        beyond = jnp.logical_and(exists(hop), crosses(hop))
+        greet(inside if hop > 0 else beyond, CORES * hop)
+        expected = expected + (inside if hop < 0 else beyond).astype(jnp.int32)
     greet(relay, span)
     greet(relay, to_tail)
     expected = expected + boxed.astype(jnp.int32) + 2 * tail.astype(jnp.int32)
     pl.semaphore_signal(barrier, inc=1, device_id=partner, device_id_type=MESH)
-    greet(jnp.logical_and(core == 0, has_below), -1)
-    greet(jnp.logical_and(core == 1, jnp.logical_and(has_above, in_line < LINE - 1)), 1)
-    expected = expected + jnp.logical_and(core == 1, has_above).astype(jnp.int32)
-    expected = expected + jnp.logical_and(core == 0, in_line > 0).astype(jnp.int32)
-
     pl.semaphore_wait(barrier, expected)
 
     for offset in (CORES - span, 2 * CORES - span):
@@ -172,6 +167,14 @@
         @pl.when(tail)
         def _(offset=offset):
             pl.semaphore_signal(here_sem.at[0], inc=1, device_id=device_at(offset), device_id_type=MESH)
+
+    for hop in (-1, -2):
+
+        @pl.when(direct(hop))
+        def _(hop=hop):
+            pl.semaphore_signal(
+                up_sem.at[-hop - 1], inc=1, device_id=device_at(CORES * hop), device_id_type=MESH
+            )
 
     loads[0].wait()
     for copy in loads[5:]:
@@ -264,22 +267,22 @@
     def _():
         box_copy.start()
 
-    for j in range(4):
+    for j in (1, 3):
 
         @pl.when(direct(HOPS[j]))
         def _(j=j):
             vol_copies[j].start()
 
     pass_copies[4].start()
-    edge_waits = jnp.logical_and(core == 0, in_line == 0)
-
-    @pl.when(jnp.logical_and(has_below, jnp.logical_not(edge_waits)))
-    def _():
-        edge_copies[0].start()
-
-    @pl.when(has_above)
-    def _():
-        edge_copies[1].start()
+    for j in (0, 2):
+
+        @pl.when(jnp.logical_and(exists(HOPS[j]), jnp.logical_not(crosses(HOPS[j]))))
+        def _(j=j):
+            pl.semaphore_wait(up_sem.at[HOPS[j] - 1], 1)
+
+        @pl.when(exists(HOPS[j]))
+        def _(j=j):
+            vol_copies[j].start()
 
     for copy in loads[1:5]:
         copy.wait()
@@ -397,9 +400,13 @@
     pass_copies[4].wait_recv()
     collect((0, 1))
 
-    @pl.when(jnp.logical_and(has_below, edge_waits))
+    @pl.when(has_below)
     def _():
         edge_copies[0].start()
+
+    @pl.when(has_above)
+    def _():
+        edge_copies[1].start()
 
     project(0, 6, 0)
     for start, width in chunks(channels, 256):
@@ -510,10 +517,10 @@
     pg_copies[0].start()
     pg_copies[2].start()
     gather(side_all, side_all)
-    hand_out((0, 2))
     backproject(side_all, last_rows, 4, 4)
     pg_copies[1].start()
     pg_copies[3].start()
+    hand_out((0, 2))
     gather(2 * side_all, tables * chip_rows)
     hand_out((1, 3))
     backproject(2 * side_all, chip_rows, 8, 2)
@@ -677,6 +684,7 @@
                 dma((1,)),
                 dma((2,)),
                 pltpu.SemaphoreType.REGULAR((1,)),
+                pltpu.SemaphoreType.REGULAR((2,)),
                 pltpu.VMEM((rows // 2, plane), bf),
                 dma((1,)),
                 dma((1,)),

time: 35.7 us -> 35.5 us (level)
  no operation moved by 1% of the time
where the time goes in v7:
time: 35.5 us; the launch traced here: 35.4 us
  Pallas kernels  34.7 us (98%)
  other arithmetic  0.67 us (2%)
    pallas_call x1, Pallas kernels, shards(): pl.pallas_call(lambda *refs: kernel(n_grp, n_view, *refs), out_shape=[jax...  34.7 us

profile of v7, /device:TPU:8, one launch (start us, length us, event | category | flops | bytes accessed | tf_op | source)
XLA Modules:
  0.0 35.4 jit_solution(6487966229355897744)
XLA Ops:
  0.0 34.7 %ct_gradient.1 = (f32[256,128]{1,0:T(8,128)S(1)}, f32[256,128]{1,0:T(8,128)S(1)}) custom-call(s32[8]{0:T(128)} %refs_0_.1, s32[4,8]{1,0:T(4,128)} %bitcast.17, s32[4,8]{1,0:T(4,128)} %bitcast.18, s32[8]{0:T(128)} %refs_3_.1, f32[256,128]{1,0:T(8,128)} %bitcast.16, bf16[2,1024,896]{2,1,0:T(8,128)(2,1)} %bitcast.14, bf16[512,896]{1,0:T(8,128)(2,1)} %bitcast.15), custom_call_target="tpu_custom_call" | custom-call | tf_op jit(solution)/shard_map/ct_gradient/pallas_call | solution.py:643
  34.7 0.7 %add.3 = f32[256,128]{1,0:T(8,128)} add(f32[256,128]{1,0:T(8,128)S(1)} %get-tuple-element.7, f32[256,128]{1,0:T(8,128)S(1)} %get-tuple-element.8) | non-fusion elementwise | flops 32768 | bytes 393216 | tf_op jit(solution)/shard_map/add | solution.py:712
